TPU v7x, 32 devices: a whole 2x2x4 slice. The times are simulated.
32 devices in a mesh: row: 8 (over z, core), col: 4 (over y, x).
Axes of the slice: x: 2, y: 2, z: 4, core: 2. Of those that a mesh axis runs over, the one named last changes fastest.
Arguments:
- queries: bfloat16 [512, 8192], P('col', 'row'), may hold values from -8 to 8
- cache_keys: bfloat16 [8, 32768, 128], P(None, ('row', 'col')), may hold values from -8 to 8
- cache_values: bfloat16 [8, 32768, 128], P(None, ('row', 'col')), may hold values from -6 to 6
- stretch_keys: bfloat16 [8, 512, 128], P(None, 'col'), may hold values from -8 to 8
- stretch_values: bfloat16 [8, 512, 128], P(None, 'col'), may hold values from -6 to 6
- block_lists: int32 [4, 8, 16], replicated, may hold values from 0 to 255, as said below
- out_weight: bfloat16 [8192, 8192], P('row', 'col'), may hold values from -0.5 to 0.5
- residual: bfloat16 [512, 8192], P('row', 'col'), may hold values from -6 to 6
- norm_gain: bfloat16 [8192], P('col'), may hold values from 0.25 to 1.75
- gate_weight: bfloat16 [8192, 28672], P('col', 'row'), may hold values from -0.0625 to 0.0625
- up_weight: bfloat16 [8192, 28672], P('col', 'row'), may hold values from -0.0625 to 0.0625
- down_weight: bfloat16 [28672, 8192], P('row', 'col'), may hold values from -0.03125 to 0.03125
Outputs:
- layer_out: bfloat16 [512, 8192], P('row', 'col')
Inputs may be any that keep to these rules, and one draw needn't show every extreme that they name: `block_lists`: each list names 16 different cache blocks; device k of row+col holds cache blocks k * (8) to (k + 1) * 8 - 1, and no two blocks of one list lie on the same device. Every list holds block 0 and block 255.
All inputs are finite; a program needn't handle non-finite values.
Results may differ from a plain program's by a relative error of at most 0.0085.
Values may be sent and summed in bfloat16 or wider, within the bound.
A program may use at most 128 MiB of HBM per device.

v0:
```python
import functools
import math

import jax
import jax.numpy as jnp
from jax import lax
from jax.experimental import pallas as pl
from jax.experimental.pallas import tpu as pltpu
from jax.sharding import PartitionSpec as P

D = 8192
KV_HEADS = 8
HEAD_DIM = 128
BLK = 128
GROUP = 8
WIDTH = 256
SLOTS = 4
MESH = pl.DeviceIdType.MESH


def feed_forward_kernel(
    peers,
    chunks,
    pieces_ref,
    squares_ref,
    gate_ref,
    up_ref,
    down_ref,
    out_ref,
    gate_buf,
    up_buf,
    down_buf,
    gate_part,
    up_part,
    gate_first,
    up_first,
    gate_mid,
    up_mid,
    gate_second,
    up_second,
    left,
    right,
    square_buf,
    factor_buf,
    total,
    gate_sem,
    up_sem,
    down_sem,
    pair_send,
    pair_recv,
    line_send,
    line_recv,
    square_send,
    square_recv,
):
    me = lax.axis_index("col")
    depth = gate_ref.shape[0]
    lines = peers // 2
    half = WIDTH // 2
    pair_me = lax.rem(me, 2)
    line_me = me // 2
    other = line_me * 2 + (1 - pair_me)

    def line(k):
        return lax.rem(line_me + k, lines)

    def remote(src, dst, send, recv, device):
        return pltpu.make_async_remote_copy(
            src_ref=src,
            dst_ref=dst,
            send_sem=send,
            recv_sem=recv,
            device_id={"col": device},
            device_id_type=MESH,
        )

    def transfers(stage, slot):
        if stage == 0:
            pair = (gate_part.at[slot, 1 - pair_me], gate_first.at[slot])
            along = [(up_part.at[slot, line(k)], up_first.at[slot, k - 1]) for k in range(1, lines)]
        elif stage == 1:
            pair = (up_mid.at[slot, 1 - pair_me], up_second.at[slot])
            along = [(gate_mid.at[slot, line(k)], gate_second.at[slot, k - 1]) for k in range(1, lines)]
        elif stage == 2:
            pair = (left.at[slot, 0, 0], left.at[slot, 0, 1])
            along = [(right.at[slot, 0, 0], right.at[slot, 0, k]) for k in range(1, lines)]
        else:
            pair = (right.at[slot, 0], right.at[slot, 1])
            along = [(left.at[slot, 0], left.at[slot, k]) for k in range(1, lines)]
        copies = [
            remote(*pair, pair_send.at[stage, slot], pair_recv.at[stage, slot], other)
        ]
        for k in range(1, lines):
            copies.append(
                remote(
                    *along[k - 1],
                    line_send.at[stage, slot, k - 1],
                    line_recv.at[stage, slot, k - 1],
                    line(k) * 2 + pair_me,
                )
            )
        return copies

    def square_copy(k):
        return remote(
            squares_ref.at[lax.rem(me + k, peers)],
            square_buf.at[k - 1],
            square_send.at[k - 1],
            square_recv.at[k - 1],
            lax.rem(me + k, peers),
        )

    def columns(j):
        return pl.ds(pl.multiple_of(j * WIDTH, WIDTH), WIDTH)

    def gate_copy(j):
        slot = lax.rem(j, 2)
        return pltpu.make_async_copy(
            gate_ref.at[:, columns(j)], gate_buf.at[slot], gate_sem.at[slot]
        )

    def up_copy(j):
        slot = lax.rem(j, 2)
        return pltpu.make_async_copy(up_ref.at[:, columns(j)], up_buf.at[slot], up_sem.at[slot])

    def down_copy(j):
        slot = lax.rem(j, 2)
        return pltpu.make_async_copy(
            down_ref.at[columns(j), :], down_buf.at[slot], down_sem.at[slot]
        )

    gate_copy(0).start()
    up_copy(0).start()
    down_copy(0).start()
    barrier = pltpu.get_barrier_semaphore()
    for k in range(1, peers):
        pl.semaphore_signal(
            barrier, inc=1, device_id={"col": lax.rem(me + k, peers)}, device_id_type=MESH
        )
    pl.semaphore_wait(barrier, peers - 1)
    for k in range(1, peers):
        square_copy(k).start()
    total[...] = jnp.zeros_like(total)

    def stage_when(i, stage):
        return pl.when((i >= stage) & (i < chunks + stage))

    def step(i, carry):
        @stage_when(i, 0)
        def _():
            @pl.when(i + 1 < chunks)
            def _():
                gate_copy(i + 1).start()
                up_copy(i + 1).start()

            slot = lax.rem(i, SLOTS)
            gate_copy(i).wait()
            product = jnp.dot(
                pieces_ref[:, :depth], gate_buf[lax.rem(i, 2)], preferred_element_type=jnp.float32
            ).astype(jnp.bfloat16)
            for b in range(peers):
                gate_part[slot, b % 2, b // 2] = product[b * BLK : (b + 1) * BLK]
            up_copy(i).wait()
            product = jnp.dot(
                pieces_ref[:, :depth], up_buf[lax.rem(i, 2)], preferred_element_type=jnp.float32
            ).astype(jnp.bfloat16)
            for b in range(peers):
                up_part[slot, b // 2, b % 2] = product[b * BLK : (b + 1) * BLK]
            for copy in transfers(0, slot):
                copy.start()

        @stage_when(i, 1)
        def _():
            slot = lax.rem(i - 1, SLOTS)
            for copy in transfers(0, slot):
                copy.wait()
            gate_mid[slot] = (
                gate_part[slot, pair_me].astype(jnp.float32) + gate_first[slot].astype(jnp.float32)
            ).astype(jnp.bfloat16)
            up_sum = up_part[slot, line_me].astype(jnp.float32)
            for k in range(1, lines):
                up_sum = up_sum + up_first[slot, k - 1].astype(jnp.float32)
            up_mid[slot] = up_sum.astype(jnp.bfloat16)
            for copy in transfers(1, slot):
                copy.start()

        @pl.when(i == 2)
        def _():
            squares = squares_ref[me]
            for k in range(1, peers):
                square_copy(k).wait()
                squares = squares + square_buf[k - 1]
            factor_buf[...] = lax.rsqrt(squares / D + 1e-05)

        @stage_when(i, 2)
        def _():
            slot = lax.rem(i - 2, SLOTS)
            for copy in transfers(1, slot):
                copy.wait()
            gate = gate_mid[slot, line_me].astype(jnp.float32)
            for k in range(1, lines):
                gate = gate + gate_second[slot, k - 1].astype(jnp.float32)
            up = up_mid[slot, pair_me].astype(jnp.float32) + up_second[slot].astype(jnp.float32)
            factor = factor_buf[:, :1]
            gate = gate * factor
            hidden = (gate / (1.0 + jnp.exp(-gate)) * (up * factor)).astype(jnp.bfloat16)
            left[slot, 0, 0] = hidden[:, :half]
            right[slot, 0, 0] = hidden[:, half:]
            for copy in transfers(2, slot):
                copy.start()

        @stage_when(i, 3)
        def _():
            slot = lax.rem(i - 3, SLOTS)
            for copy in transfers(2, slot):
                copy.wait()
            for copy in transfers(3, slot):
                copy.start()

        @stage_when(i, 4)
        def _():
            j = i - 4
            slot = lax.rem(j, SLOTS)

            @pl.when(j + 1 < chunks)
            def _():
                down_copy(j + 1).start()

            down_copy(j).wait()
            for copy in transfers(3, slot):
                copy.wait()
            gathered = jnp.concatenate(
                [
                    jnp.concatenate([left[slot, k, p], right[slot, p, k]], axis=1)
                    for p in range(2)
                    for k in range(lines)
                ],
                axis=0,
            )
            out_width = total.shape[1]
            tile = min(512, out_width)
            for start in range(0, out_width, tile):
                total[:, start : start + tile] += jnp.dot(
                    gathered,
                    down_buf[lax.rem(j, 2), :, start : start + tile],
                    preferred_element_type=jnp.float32,
                )

        return carry

    lax.fori_loop(0, chunks + 4, step, 0)
    for p in range(2):
        for k in range(lines):
            owner = line(lines - k) * 2 + lax.rem(pair_me + p, 2)
            first = (p * lines + k) * BLK
            out_ref[owner] = total[first : first + BLK, :].astype(jnp.bfloat16)


def feed_forward(pieces, squares, gate_weight, up_weight, down_weight):
    peers = lax.axis_size("col")
    lines = peers // 2
    depth, hidden_width = gate_weight.shape
    out_width = down_weight.shape[1]
    chunks = hidden_width // WIDTH
    vmem = pl.BlockSpec(memory_space=pltpu.VMEM)
    hbm = pl.BlockSpec(memory_space=pl.ANY)
    dma = pltpu.SemaphoreType.DMA

    def held(*shape):
        return pltpu.VMEM(shape, jnp.bfloat16)

    return pl.pallas_call(
        functools.partial(feed_forward_kernel, peers, chunks),
        out_shape=jax.ShapeDtypeStruct((peers, BLK, out_width), jnp.bfloat16),
        in_specs=[vmem, vmem, hbm, hbm, hbm],
        out_specs=vmem,
        scratch_shapes=[
            held(2, depth, WIDTH),
            held(2, depth, WIDTH),
            held(2, WIDTH, out_width),
            held(SLOTS, 2, lines, BLK, WIDTH),
            held(SLOTS, lines, 2, BLK, WIDTH),
            held(SLOTS, lines, BLK, WIDTH),
            held(SLOTS, lines - 1, 2, BLK, WIDTH),
            held(SLOTS, lines, BLK, WIDTH),
            held(SLOTS, 2, BLK, WIDTH),
            held(SLOTS, lines - 1, BLK, WIDTH),
            held(SLOTS, BLK, WIDTH),
            held(SLOTS, lines, 2, BLK, WIDTH // 2),
            held(SLOTS, 2, lines, BLK, WIDTH // 2),
            pltpu.VMEM((peers - 1, BLK, 128), jnp.float32),
            pltpu.VMEM((BLK, 128), jnp.float32),
            pltpu.VMEM((peers * BLK, out_width), jnp.float32),
            dma((2,)),
            dma((2,)),
            dma((2,)),
            dma((4, SLOTS)),
            dma((4, SLOTS)),
            dma((4, SLOTS, lines - 1)),
            dma((4, SLOTS, lines - 1)),
            dma((peers - 1,)),
            dma((peers - 1,)),
        ],
        compiler_params=pltpu.CompilerParams(
            collective_id=0, has_side_effects=True, vmem_limit_bytes=48 * 1024 * 1024
        ),
    )(pieces, squares, gate_weight, up_weight, down_weight)


def project_kernel(peers, own_ref, weight_ref, out_ref, gathered, weight_buf, weight_sem, send, recv):
    me = lax.axis_index("col")

    def copy_to(k):
        return pltpu.make_async_remote_copy(
            src_ref=own_ref,
            dst_ref=gathered.at[k - 1],
            send_sem=send.at[k - 1],
            recv_sem=recv.at[k - 1],
            device_id={"col": lax.rem(me + k, peers)},
            device_id_type=MESH,
        )

    weights = pltpu.make_async_copy(weight_ref, weight_buf, weight_sem)
    weights.start()
    barrier = pltpu.get_barrier_semaphore()
    for k in range(1, peers):
        pl.semaphore_signal(
            barrier, inc=1, device_id={"col": lax.rem(me + k, peers)}, device_id_type=MESH
        )
    pl.semaphore_wait(barrier, peers - 1)
    for k in range(1, peers):
        copy_to(k).start()
    weights.wait()
    out_width = weight_buf.shape[1]
    tile = min(512, out_width)
    for k in range(peers):
        if k > 0:
            copy_to(k).wait()
            rows = gathered[k - 1]
        else:
            rows = own_ref[...]
        owner = lax.rem(me + peers - k, peers)
        for start in range(0, out_width, tile):
            out_ref[owner, :, start : start + tile] = jnp.dot(
                rows, weight_buf[:, start : start + tile], preferred_element_type=jnp.float32
            ).astype(jnp.bfloat16)


def project(attended, out_weight):
    peers = lax.axis_size("col")
    width, out_width = out_weight.shape
    dma = pltpu.SemaphoreType.DMA
    return pl.pallas_call(
        functools.partial(project_kernel, peers),
        out_shape=jax.ShapeDtypeStruct((peers, BLK, out_width), jnp.bfloat16),
        in_specs=[pl.BlockSpec(memory_space=pltpu.VMEM), pl.BlockSpec(memory_space=pl.ANY)],
        out_specs=pl.BlockSpec(memory_space=pltpu.VMEM),
        scratch_shapes=[
            pltpu.VMEM((peers - 1, BLK, width), jnp.bfloat16),
            pltpu.VMEM((width, out_width), jnp.bfloat16),
            dma,
            dma((peers - 1,)),
            dma((peers - 1,)),
        ],
        compiler_params=pltpu.CompilerParams(
            collective_id=1, has_side_effects=True, vmem_limit_bytes=48 * 1024 * 1024
        ),
    )(attended, out_weight)


def row_sum_kernel(lines, part_ref, out_ref, first, mid, second, pair_send, pair_recv, line_send, line_recv):
    me = lax.axis_index("row")
    pair_me = lax.rem(me, 2)
    line_me = me // 2
    other = line_me * 2 + (1 - pair_me)
    pieces, _, _, width = first.shape

    def line(k):
        return lax.rem(line_me + k, lines)

    def pair_copy(c):
        return pltpu.make_async_remote_copy(
            src_ref=part_ref.at[:, 1 - pair_me, :, c * width : (c + 1) * width],
            dst_ref=first.at[c],
            send_sem=pair_send.at[c],
            recv_sem=pair_recv.at[c],
            device_id={"row": other},
            device_id_type=MESH,
        )

    def line_copy(c, k):
        return pltpu.make_async_remote_copy(
            src_ref=mid.at[c, line(k)],
            dst_ref=second.at[c, k - 1],
            send_sem=line_send.at[c, k - 1],
            recv_sem=line_recv.at[c, k - 1],
            device_id={"row": line(k) * 2 + pair_me},
            device_id_type=MESH,
        )

    barrier = pltpu.get_barrier_semaphore()
    pl.semaphore_signal(barrier, inc=1, device_id={"row": other}, device_id_type=MESH)
    for k in range(1, lines):
        pl.semaphore_signal(
            barrier, inc=1, device_id={"row": line(k) * 2 + pair_me}, device_id_type=MESH
        )
    pl.semaphore_wait(barrier, lines)
    for c in range(pieces):
        pair_copy(c).start()
    for c in range(pieces):
        pair_copy(c).wait()
        own = part_ref[:, pair_me, :, c * width : (c + 1) * width]
        mid[c] = (own.astype(jnp.float32) + first[c].astype(jnp.float32)).astype(jnp.bfloat16)
        for k in range(1, lines):
            line_copy(c, k).start()
    for c in range(pieces):
        result = mid[c, line_me].astype(jnp.float32)
        for k in range(1, lines):
            line_copy(c, k).wait()
            result = result + second[c, k - 1].astype(jnp.float32)
        out_ref[:, c * width : (c + 1) * width] = result


def row_sum(partial, collective_id):
    rows = lax.axis_size("row")
    lines = rows // 2
    width = partial.shape[-1]
    tokens = partial.shape[0] * partial.shape[1] // rows
    pieces = 4
    part = width // pieces
    vmem = pl.BlockSpec(memory_space=pltpu.VMEM)
    dma = pltpu.SemaphoreType.DMA
    return pl.pallas_call(
        functools.partial(row_sum_kernel, lines),
        out_shape=jax.ShapeDtypeStruct((tokens, width), jnp.float32),
        in_specs=[vmem],
        out_specs=vmem,
        scratch_shapes=[
            pltpu.VMEM((pieces, lines, tokens, part), jnp.bfloat16),
            pltpu.VMEM((pieces, lines, tokens, part), jnp.bfloat16),
            pltpu.VMEM((pieces, lines - 1, tokens, part), jnp.bfloat16),
            dma((pieces,)),
            dma((pieces,)),
            dma((pieces, lines - 1)),
            dma((pieces, lines - 1)),
        ],
        compiler_params=pltpu.CompilerParams(
            collective_id=collective_id, has_side_effects=True, vmem_limit_bytes=32 * 1024 * 1024
        ),
    )(partial.reshape(lines, 2, tokens, width))


def local(
    queries,
    cache_keys,
    cache_values,
    stretch_keys,
    stretch_values,
    block_lists,
    out_weight,
    residual,
    norm_gain,
    gate_weight,
    up_weight,
    down_weight,
):
    row_count = lax.axis_size("row")
    col_count = lax.axis_size("col")
    row_index = lax.axis_index("row")
    col_index = lax.axis_index("col")
    device_count = row_count * col_count
    my_index = row_index * col_count + col_index
    local_blocks = cache_keys.shape[1] // BLK
    heads_here = queries.shape[1] // HEAD_DIM
    list_length = block_lists.shape[2]
    my_group = row_index * heads_here // GROUP
    scaling = 1.0 / math.sqrt(HEAD_DIM)
    targets = jnp.arange(device_count, dtype=jnp.int32)
    target_group = targets // col_count * heads_here // GROUP
    target_lists = block_lists[targets % col_count, target_group]
    holders = target_lists // local_blocks
    matched = holders == my_index
    found_any = jnp.any(matched, axis=1)
    within = jnp.sum(jnp.where(matched, target_lists % local_blocks, 0), axis=1)
    source_rows = target_group * local_blocks + within
    flat_keys = cache_keys.reshape(KV_HEADS * local_blocks, BLK, HEAD_DIM)
    flat_values = cache_values.reshape(KV_HEADS * local_blocks, BLK, HEAD_DIM)
    outgoing = jnp.concatenate([flat_keys[source_rows], flat_values[source_rows]], axis=2)
    outgoing = jnp.where(found_any[:, None, None], outgoing, jnp.zeros_like(outgoing))
    arrived = lax.all_to_all(outgoing, ("row", "col"), split_axis=0, concat_axis=0, tiled=True)
    my_list = block_lists[col_index, my_group]
    fetched = arrived[my_list // local_blocks].reshape(list_length * BLK, 2 * HEAD_DIM)
    far_keys = fetched[:, :HEAD_DIM]
    far_values = fetched[:, HEAD_DIM:]
    query_rows = queries.reshape(BLK * heads_here, HEAD_DIM)
    far_scores = jnp.dot(query_rows, far_keys.T, preferred_element_type=jnp.float32) * scaling
    run_max = jnp.max(far_scores, axis=1)
    far_exp = jnp.exp(far_scores - run_max[:, None])
    run_sum = jnp.sum(far_exp, axis=1)
    run_acc = jnp.dot(far_exp.astype(jnp.bfloat16), far_values, preferred_element_type=jnp.float32)
    query_pos = col_index * BLK + jnp.arange(BLK * heads_here, dtype=jnp.int32) // heads_here
    own = jnp.concatenate([stretch_keys, stretch_values], axis=2)
    own = lax.dynamic_index_in_dim(own, my_group, 0, keepdims=False)
    piece = lax.all_gather(own, "col", axis=0, tiled=True)
    piece_keys = piece[:, :HEAD_DIM]
    piece_values = piece[:, HEAD_DIM:]
    scores = jnp.dot(query_rows, piece_keys.T, preferred_element_type=jnp.float32) * scaling
    key_pos = jnp.arange(piece_keys.shape[0], dtype=jnp.int32)
    allowed = key_pos[None, :] <= query_pos[:, None]
    scores = jnp.where(allowed, scores, -1e30)
    new_max = jnp.maximum(run_max, jnp.max(scores, axis=1))
    decays = jnp.exp(run_max - new_max)
    weights = jnp.where(allowed, jnp.exp(scores - new_max[:, None]), 0.0)
    new_sum = run_sum * decays + jnp.sum(weights, axis=1)
    new_acc = run_acc * decays[:, None] + jnp.dot(
        weights.astype(jnp.bfloat16), piece_values, preferred_element_type=jnp.float32
    )
    attended = (new_acc / new_sum[:, None]).astype(jnp.bfloat16).reshape(BLK, heads_here * HEAD_DIM)
    projected = row_sum(project(attended, out_weight), 2)
    stream = residual.astype(jnp.float32) + projected.astype(jnp.float32)
    scaled = (stream * norm_gain.astype(jnp.float32)).astype(jnp.bfloat16)
    rest = jnp.sum(stream * stream, axis=1, keepdims=True)
    terms = []
    for _ in range(3):
        term = lax.reduce_precision(rest, exponent_bits=8, mantissa_bits=7)
        terms.append(term)
        rest = rest - term
    riders = jnp.concatenate(terms + [jnp.zeros((rest.shape[0], 125), jnp.float32)], axis=1)
    outgoing_piece = jnp.concatenate([scaled, riders.astype(jnp.bfloat16)], axis=1)
    pieces = lax.all_gather(outgoing_piece, "row", axis=0, tiled=True)
    squares = jnp.sum(pieces[:, scaled.shape[1] :].astype(jnp.float32), axis=1, keepdims=True)
    squares = jnp.broadcast_to(squares, (squares.shape[0], 128)).reshape(col_count, BLK, 128)
    down_terms = feed_forward(pieces, squares, gate_weight, up_weight, down_weight)
    mlp_part = row_sum(down_terms, 3)
    return (stream + mlp_part.astype(jnp.float32)).astype(jnp.bfloat16)


def solution(mesh):
    in_specs = (
        P("col", "row"),
        P(None, ("row", "col"), None),
        P(None, ("row", "col"), None),
        P(None, "col", None),
        P(None, "col", None),
        P(),
        P("row", "col"),
        P("row", "col"),
        P("col"),
        P("col", "row"),
        P("col", "row"),
        P("row", "col"),
    )
    out_specs = P("row", "col")
    return jax.shard_map(local, mesh=mesh, in_specs=in_specs, out_specs=out_specs, check_vma=False)
```

profile of v0, /device:TPU:0, one launch (start us, length us, event | category | flops | bytes accessed | tf_op | source)
XLA Modules:
  0.0 288.3 jit_solution(10123626797566761036)
XLA Ops:
  6.5 0.0 copy-start
  6.6 1.5 gather_fusion
  8.1 0.1 fusion.51
  8.2 0.1 fusion.29
  8.4 0.0 copy-done
  8.4 0.7 gather_fusion.1
  9.1 2.3 gather_fusion.2
  11.5 2.1 maximum_select_fusion
  13.6 7.3 %all-to-all-start = ((bf16[32,128,256]{2,1,0:T(8,128)(2,1)}), bf16[32,128,256]{2,1,0:T(8,128)(2,1)S(1)}, u32[]{:S(2)}, u32[]{:S(2)}) async-start(bf16[32,128,256]{2,1,0:T(8,128)(2,1)} %maximum_select_fusion), calls=%async_computation | async-start | bytes 4194304 | tf_op jit(solution)/shard_map/all_to_all | solution.py:490
  20.9 0.0 all-gather.3.cloned.1.call-start
  21.0 0.0 copy-done.7
  21.0 0.1 reshape.316
  21.1 0.0 copy-done.10
  21.1 0.0 copy-done.8
  21.1 0.0 copy-done.9
  21.2 21.1 %all-gather = bf16[1,512,256]{2,1,0:T(8,128)(2,1)S(1)} all-gather(bf16[1,128,256]{2,1,0:T(8,128)(2,1)S(1)} %fusion.24), channel_id=2, replica_groups=mesh['row'=8,'col'=4] {'col'}, dimensions={1}, use_global_device_ids=true | all-gather | bytes 327680 | tf_op jit(solution)/shard_map/all_gather | solution.py:504
  42.3 0.7 fusion.44
  43.0 0.0 copy-done.5
  43.0 1.8 fusion.4
  44.8 24.8 %all-to-all-done = bf16[32,128,256]{2,1,0:T(8,128)(2,1)S(1)} async-done(((bf16[32,128,256]{2,1,0:T(8,128)(2,1)}), bf16[32,128,256]{2,1,0:T(8,128)(2,1)S(1)}, u32[]{:S(2)}, u32[]{:S(2)}) %all-to-all-start) | async-done | bytes 2097184 | tf_op jit(solution)/shard_map/all_to_all | solution.py:490
  69.6 0.6 gather_fusion.3
  70.2 1.3 multiply_reduce_fusion
  71.5 0.0 copy-start.3
  71.5 1.4 fusion
  72.9 0.1 copy-done.3
  73.1 0.6 fusion.6
  73.7 0.0 copy-start.6
  73.7 1.5 fusion.8
  75.2 0.0 copy-done.6
  75.2 0.8 fusion.11
  76.0 0.1 reshape.317.own_ref
  76.1 15.9 %shard_map.118 = bf16[4,128,2048]{2,1,0:T(8,128)(2,1)S(1)} custom-call(bf16[128,1024]{1,0:T(8,128)(2,1)S(1)} %reshape.317.own_ref, bf16[1024,2048]{1,0:T(8,128)(2,1)} %weight_ref.1), custom_call_target="tpu_custom_call" | custom-call | tf_op jit(solution)/shard_map/pallas_call | solution.py:353
  92.0 0.0 copy-start.4
  92.0 27.3 %shard_map.119 = f32[64,2048]{1,0:T(8,128)S(1)} custom-call(bf16[4,2,64,2048]{3,2,1,0:T(8,128)(2,1)S(1)} %bitcast.42), custom_call_target="tpu_custom_call" | custom-call | tf_op jit(solution)/shard_map/pallas_call | solution.py:433
  119.3 0.2 multiply_reduce_fusion.1
  119.5 0.1 copy.16
  119.6 0.1 copy.15
  119.7 0.1 copy.17
  119.9 0.8 concatenate.18
  120.7 0.0 all-gather.3.cloned.1.call-update
  120.7 30.9 %all-gather.3.cloned.1.call-done.pieces_ref = bf16[512,2176]{1,0:T(8,128)(2,1)} async-done(((bf16[64,2176]{1,0:T(8,128)(2,1)}), bf16[512,2176]{1,0:T(8,128)(2,1)}) %all-gather.3.cloned.1.call-update) | async-done | bytes 2228240 | tf_op jit(solution)/shard_map/all_gather | solution.py:530
  151.6 1.0 convert_reduce_fusion
  152.6 0.1 broadcast_in_dim.51.squares_ref
  152.7 1.6 copy-done.2
  154.4 99.0 %shard_map.120 = bf16[4,128,2048]{2,1,0:T(8,128)(2,1)S(1)} custom-call(bf16[512,2176]{1,0:T(8,128)(2,1)S(1)} %copy-done.2, f32[4,128,128]{2,1,0:T(8,128)S(1)} %broadcast_in_dim.51.squares_ref, bf16[2048,3584]{1,0:T(8,128)(2,1)} %gate_ref.1, bf16[2048,3584]{1,0:T(8,128)(2,1)} %up_ref.1, bf16[3584,2048]{1,0:T(8,128)(2,1)} %down_ref.1), custom_call_target="tpu_custom_call" | custom-call | tf_op jit(solution)/shard_map/pallas_call | solution.py:272
  253.4 0.0 copy-start.1
  253.4 27.2 %shard_map.121 = f32[64,2048]{1,0:T(8,128)S(1)} custom-call(bf16[4,2,64,2048]{3,2,1,0:T(8,128)(2,1)S(1)} %bitcast.41), custom_call_target="tpu_custom_call" | custom-call | tf_op jit(solution)/shard_map/pallas_call | solution.py:433
  280.7 0.8 add_convert_fusion
  (20 shorter events, 0.1 us)
Async XLA Ops:
  6.5 1.8 copy-start
  13.6 7.4 %copy-start.7 = (bf16[128,1024]{1,0:T(8,128)(2,1)S(1)}, bf16[128,1024]{1,0:T(8,128)(2,1)}, u32[]{:S(2)}) copy-start(bf16[128,1024]{1,0:T(8,128)(2,1)} %param.12) | copy-start | bytes 786436
  13.6 7.5 %copy-start.10 = (bf16[2048]{0:T(1024)(128)(2,1)S(1)}, bf16[2048]{0:T(1024)(128)(2,1)}, u32[]{:S(2)}) copy-start(bf16[2048]{0:T(1024)(128)(2,1)} %param.20) | copy-start | bytes 12292
  13.6 7.6 %copy-start.8 = (bf16[8,128,128]{2,1,0:T(8,128)(2,1)S(1)}, bf16[8,128,128]{2,1,0:T(8,128)(2,1)}, u32[]{:S(2)}) copy-start(bf16[8,128,128]{2,1,0:T(8,128)(2,1)} %param.15) | copy-start | bytes 786436
  13.6 7.6 %copy-start.9 = (bf16[8,128,128]{2,1,0:T(8,128)(2,1)S(1)}, bf16[8,128,128]{2,1,0:T(8,128)(2,1)}, u32[]{:S(2)}) copy-start(bf16[8,128,128]{2,1,0:T(8,128)(2,1)} %param.16) | copy-start | bytes 786436
  13.6 56.0 %all-to-all-start = ((bf16[32,128,256]{2,1,0:T(8,128)(2,1)}), bf16[32,128,256]{2,1,0:T(8,128)(2,1)S(1)}, u32[]{:S(2)}, u32[]{:S(2)}) async-start(bf16[32,128,256]{2,1,0:T(8,128)(2,1)} %maximum_select_fusion), calls=%async_computation | async-start | bytes 4194304 | tf_op jit(solution)/shard_map/all_to_all | solution.py:490
  20.9 130.7 %all-gather.3.cloned.1.call-start = ((), (), s32[]{:S(2)}) async-start(), calls=%async_computation.1 | async-start | bytes 2506752 | tf_op jit(solution)/shard_map/all_gather | solution.py:530
  42.3 0.7 copy-start.5
  71.5 1.6 copy-start.3
  73.7 1.5 copy-start.6
  92.0 27.3 %copy-start.4 = (bf16[64,2048]{1,0:T(8,128)(2,1)S(1)}, bf16[64,2048]{1,0:T(8,128)(2,1)}, u32[]{:S(2)}) copy-start(bf16[64,2048]{1,0:T(8,128)(2,1)} %param.19) | copy-start | bytes 786436
  152.7 1.6 copy-start.2
  253.4 28.0 %copy-start.1 = (bf16[8,1024,128]{2,1,0:T(8,128)(2,1)S(1)}, bf16[8,1024,128]{2,1,0:T(8,128)(2,1)}, u32[]{:S(2)}) copy-start(bf16[8,1024,128]{2,1,0:T(8,128)(2,1)} %param.13) | copy-start | bytes 6291460
Sparse Core Ops, SparseCore 0:
  120.8 30.7 all-gather.2
where the time goes:
time: 289 us; the launch traced here: 288 us
  Pallas kernels  169 us (58%)
  waiting for transfers between devices  55.7 us (19%)
  blocking collectives  21.1 us (7%)
  between operations  13.7 us (5%)
  local copies, waits for them, and re-layouts  8.52 us (3%)
  starting transfers between devices  7.37 us (3%)
  other arithmetic  7.13 us (2%)
  matrix products  5.29 us (2%)
    pallas_call x1, Pallas kernels, feed_forward(): pl.pallas_call(functools.partial(feed_forward_kernel, peers, chunks), out...  99 us
    pallas_call x2, Pallas kernels, row_sum(): pl.pallas_call(functools.partial(row_sum_kernel, lines), out_shape=jax.Sh...  54.5 us
    all_gather x1, waiting for transfers between devices, local(): pieces = lax.all_gather(outgoing_piece, 'row', axis=0, tiled=True)  30.9 us
    all_to_all x1, waiting for transfers between devices, local(): lax.all_to_all(outgoing, ('row', 'col'), split_axis=0, concat_axis=0, til...  24.8 us
    all_gather x1, blocking collectives, local(): piece = lax.all_gather(own, 'col', axis=0, tiled=True)  21.1 us
    pallas_call x1, Pallas kernels, project(): pl.pallas_call(functools.partial(project_kernel, peers), out_shape=jax.Sh...  15.9 us
    all_to_all x1, starting transfers between devices, local(): lax.all_to_all(outgoing, ('row', 'col'), split_axis=0, concat_axis=0, til...  7.33 us
  transfers between devices with their start and end apart: 2, of which 2 were waited for; matrix products, arithmetic and copies ran while one was open for 1% of the time, Pallas kernels for 0%

commit v1 on v0

v1 whole, which is shorter than its diff:
```python
import functools
import math

import jax
import jax.numpy as jnp
from jax import lax
from jax.experimental import pallas as pl
from jax.experimental.pallas import tpu as pltpu
from jax.sharding import PartitionSpec as P

KV_HEADS = 8
HEAD_DIM = 128
BLK = 128
GROUP = 8
SLOTS = 4
MESH = pl.DeviceIdType.MESH
NC = 4
STEPS = 7


def tail_kernel(
    cols,
    rows,
    att_ref,
    wo_ref,
    res_ref,
    gain_ref,
    gate_ref,
    up_ref,
    down_ref,
    out_ref,
    gate_buf,
    up_buf,
    down_buf,
    att_buf,
    part,
    first,
    mid,
    second,
    stream,
    square_own,
    square_buf,
    pieces,
    gate_part,
    up_part,
    gate_first,
    up_first,
    gate_mid,
    up_mid,
    gate_second,
    up_second,
    left,
    right,
    total,
    gate_sem,
    up_sem,
    down_sem,
    wo_sem,
    att_send,
    att_recv,
    rs_pair_send,
    rs_pair_recv,
    rs_line_send,
    rs_line_recv,
    square_send,
    square_recv,
    ag_line_send,
    ag_line_recv,
    ag_pair_send,
    ag_pair_recv,
    pair_send,
    pair_recv,
    line_send,
    line_recv,
):
    col = lax.axis_index("col")
    row = lax.axis_index("row")
    steps = gate_buf.shape[0]
    wide = gate_buf.shape[2]
    half = wide // 2
    share = gate_part.shape[3]
    _, toks, width = out_ref.shape
    many = cols * share
    spare = wo_ref.shape[0] // wide
    tile = min(512, width)
    col_lines = cols // 2
    pair_me = lax.rem(col, 2)
    line_me = col // 2
    col_other = line_me * 2 + (1 - pair_me)
    row_lines = rows // 2
    core = lax.rem(row, 2)
    depth_me = row // 2
    row_other = depth_me * 2 + (1 - core)

    def line(k):
        return lax.rem(line_me + k, col_lines)

    def layer(k):
        return lax.rem(depth_me + k, row_lines)

    def remote(src, dst, send, recv, axis, device):
        return pltpu.make_async_remote_copy(
            src_ref=src,
            dst_ref=dst,
            send_sem=send,
            recv_sem=recv,
            device_id={axis: device},
            device_id_type=MESH,
        )

    def gate_copy(j):
        return pltpu.make_async_copy(
            gate_ref.at[:, pl.ds(pl.multiple_of(j * wide, wide), wide)], gate_buf.at[j], gate_sem.at[j]
        )

    def up_copy(j):
        return pltpu.make_async_copy(
            up_ref.at[:, pl.ds(pl.multiple_of(j * wide, wide), wide)], up_buf.at[j], up_sem.at[j]
        )

    def down_copy(j):
        return pltpu.make_async_copy(
            down_ref.at[pl.ds(pl.multiple_of(j * wide, wide), wide), :], down_buf.at[j], down_sem.at[j]
        )

    def wo_copy(p):
        return pltpu.make_async_copy(
            wo_ref.at[p * wide : (p + 1) * wide, :], down_buf.at[steps - spare + p], wo_sem.at[p]
        )

    def att_copy(q, k):
        return remote(
            att_ref.at[:, q * toks : (q + 1) * toks, :],
            att_buf.at[q, col],
            att_send.at[q, k - 1],
            att_recv.at[q, k - 1],
            "col",
            lax.rem(col + k, cols),
        )

    def rs_pair(w, q):
        return remote(
            part.at[w, q, :, 1 - core],
            first.at[w, q],
            rs_pair_send.at[w, q],
            rs_pair_recv.at[w, q],
            "row",
            row_other,
        )

    def rs_line(w, q, k):
        return remote(
            mid.at[w, q, layer(k)],
            second.at[w, q, k - 1],
            rs_line_send.at[w, q, k - 1],
            rs_line_recv.at[w, q, k - 1],
            "row",
            layer(k) * 2 + core,
        )

    def rs_middle(w, q):
        rs_pair(w, q).wait()
        for d in range(row_lines):
            mid[w, q, d] = (
                part[w, q, d, core].astype(jnp.float32) + first[w, q, d].astype(jnp.float32)
            ).astype(jnp.bfloat16)

    def rs_lines_start(w, q):
        for k in range(1, row_lines):
            rs_line(w, q, k).start()

    def rs_finish(w, q):
        result = mid[w, q, depth_me].astype(jnp.float32)
        for k in range(1, row_lines):
            rs_line(w, q, k).wait()
            result = result + second[w, q, k - 1].astype(jnp.float32)
        return result

    def square_copy(q, k):
        return remote(
            square_own.at[q],
            square_buf.at[q, k - 1],
            square_send.at[q, k - 1],
            square_recv.at[q, k - 1],
            "col",
            lax.rem(col + k, cols),
        )

    def stream_step(q):
        value = rs_finish(0, q) + res_ref[q].astype(jnp.float32)
        stream[q] = value
        squares = jnp.sum(value * value, axis=1, keepdims=True)
        square_own[q] = jnp.broadcast_to(squares, (toks, 128))
        for k in range(1, cols):
            square_copy(q, k).start()

    def ag_line(q, k):
        return remote(
            pieces.at[q, depth_me, core],
            pieces.at[q, depth_me, core],
            ag_line_send.at[q, k - 1],
            ag_line_recv.at[q, k - 1],
            "row",
            layer(k) * 2 + core,
        )

    def ag_pair(q, k):
        owner = layer(row_lines - k)
        return remote(
            pieces.at[q, owner, core],
            pieces.at[q, owner, core],
            ag_pair_send.at[q, k],
            ag_pair_recv.at[q, k],
            "row",
            row_other,
        )

    def norm_step(q):
        squares = square_own[q]
        for k in range(1, cols):
            square_copy(q, k).wait()
            squares = squares + square_buf[q, k - 1]
        factor = lax.rsqrt(squares / (width * cols) + 1e-05)[:, :1]
        pieces[q, depth_me, core] = (stream[q] * factor * gain_ref[...].astype(jnp.float32)).astype(
            jnp.bfloat16
        )
        for k in range(1, row_lines):
            ag_line(q, k).start()
        ag_pair(q, 0).start()

    def ag_forward(q):
        for k in range(1, row_lines):
            ag_line(q, k).wait()
            ag_pair(q, k).start()

    def ag_done(q):
        for k in range(row_lines):
            ag_pair(q, k).wait()

    def transfers(stage, slot):
        if stage == 0:
            pair = (gate_part.at[slot, 1 - pair_me], gate_first.at[slot])
            along = [(up_part.at[slot, line(k)], up_first.at[slot, k - 1]) for k in range(1, col_lines)]
        elif stage == 1:
            pair = (up_mid.at[slot, 1 - pair_me], up_second.at[slot])
            along = [(gate_mid.at[slot, line(k)], gate_second.at[slot, k - 1]) for k in range(1, col_lines)]
        elif stage == 2:
            pair = (left.at[slot, 0, 0], left.at[slot, 0, 1])
            along = [(right.at[slot, 0, 0], right.at[slot, 0, k]) for k in range(1, col_lines)]
        else:
            pair = (right.at[slot, 0], right.at[slot, 1])
            along = [(left.at[slot, 0], left.at[slot, k]) for k in range(1, col_lines)]
        copies = [
            remote(*pair, pair_send.at[stage, slot], pair_recv.at[stage, slot], "col", col_other)
        ]
        for k in range(1, col_lines):
            copies.append(
                remote(
                    *along[k - 1],
                    line_send.at[stage, slot, k - 1],
                    line_recv.at[stage, slot, k - 1],
                    "col",
                    line(k) * 2 + pair_me,
                )
            )
        return copies

    for p in range(spare):
        wo_copy(p).start()
    for j in range(steps):
        gate_copy(j).start()
        up_copy(j).start()
        if j < steps - spare:
            down_copy(j).start()
    barrier = pltpu.get_barrier_semaphore()
    for k in range(1, cols):
        pl.semaphore_signal(
            barrier, inc=1, device_id={"col": lax.rem(col + k, cols)}, device_id_type=MESH
        )
    pl.semaphore_signal(barrier, inc=1, device_id={"row": row_other}, device_id_type=MESH)
    for k in range(1, row_lines):
        pl.semaphore_signal(
            barrier, inc=1, device_id={"row": layer(k) * 2 + core}, device_id_type=MESH
        )
    pl.semaphore_wait(barrier, cols - 1 + row_lines)
    for q in range(NC):
        for k in range(1, cols):
            att_copy(q, k).start()
    total[...] = jnp.zeros_like(total)
    for p in range(spare):
        wo_copy(p).wait()

    for q in range(NC):
        att_buf[q, col] = att_ref[:, q * toks : (q + 1) * toks, :]
        for k in range(1, cols):
            att_copy(q, k).wait()
        inputs = att_buf[q].reshape(many, att_buf.shape[-1])
        for start in range(0, width, tile):
            product = jnp.zeros((many, tile), jnp.float32)
            for p in range(spare):
                product = product + jnp.dot(
                    inputs[:, p * wide : (p + 1) * wide],
                    down_buf[steps - spare + p, :, start : start + tile],
                    preferred_element_type=jnp.float32,
                )
            part[0, q, :, :, :, start : start + tile] = product.astype(jnp.bfloat16).reshape(
                row_lines, 2, toks, tile
            )
        rs_pair(0, q).start()
        rs_middle(0, q)
        if q == 0:
            rs_lines_start(0, 0)
    for j in range(steps - spare, steps):
        down_copy(j).start()
    stream_step(0)
    norm_step(0)
    if NC > 1:
        rs_lines_start(0, 1)
    ag_forward(0)

    chunks = NC * steps

    def stage_when(i, stage):
        return pl.when((i >= stage) & (i < chunks + stage))

    def iteration(i, carry):
        q_now = i // steps
        j_now = lax.rem(i, steps)

        @pl.when((j_now == 0) & (q_now < NC))
        def _():
            ag_done(q_now)

        @stage_when(i, 0)
        def _():
            @pl.when(i < steps)
            def _():
                gate_copy(i).wait()
                up_copy(i).wait()

            slot = lax.rem(i, SLOTS)
            inputs = pieces[q_now].reshape(many, pieces.shape[-1])
            product = jnp.dot(inputs, gate_buf[j_now], preferred_element_type=jnp.float32).astype(jnp.bfloat16)
            for b in range(cols):
                gate_part[slot, b % 2, b // 2] = product[b * share : (b + 1) * share]
            product = jnp.dot(inputs, up_buf[j_now], preferred_element_type=jnp.float32).astype(jnp.bfloat16)
            for b in range(cols):
                up_part[slot, b // 2, b % 2] = product[b * share : (b + 1) * share]
            for copy in transfers(0, slot):
                copy.start()

        @stage_when(i, 1)
        def _():
            slot = lax.rem(i - 1, SLOTS)
            for copy in transfers(0, slot):
                copy.wait()
            gate_mid[slot] = (
                gate_part[slot, pair_me].astype(jnp.float32) + gate_first[slot].astype(jnp.float32)
            ).astype(jnp.bfloat16)
            up_sum = up_part[slot, line_me].astype(jnp.float32)
            for k in range(1, col_lines):
                up_sum = up_sum + up_first[slot, k - 1].astype(jnp.float32)
            up_mid[slot] = up_sum.astype(jnp.bfloat16)
            for copy in transfers(1, slot):
                copy.start()

        @stage_when(i, 2)
        def _():
            slot = lax.rem(i - 2, SLOTS)
            for copy in transfers(1, slot):
                copy.wait()
            gate = gate_mid[slot, line_me].astype(jnp.float32)
            for k in range(1, col_lines):
                gate = gate + gate_second[slot, k - 1].astype(jnp.float32)
            up = up_mid[slot, pair_me].astype(jnp.float32) + up_second[slot].astype(jnp.float32)
            hidden = (gate / (1.0 + jnp.exp(-gate)) * up).astype(jnp.bfloat16)
            left[slot, 0, 0] = hidden[:, :half]
            right[slot, 0, 0] = hidden[:, half:]
            for copy in transfers(2, slot):
                copy.start()

        @stage_when(i, 3)
        def _():
            slot = lax.rem(i - 3, SLOTS)
            for copy in transfers(2, slot):
                copy.wait()
            for copy in transfers(3, slot):
                copy.start()

        @stage_when(i, 4)
        def _():
            j = lax.rem(i - 4, steps)
            slot = lax.rem(i - 4, SLOTS)

            @pl.when(i - 4 < steps)
            def _():
                down_copy(i - 4).wait()

            for copy in transfers(3, slot):
                copy.wait()
            gathered = jnp.concatenate(
                [
                    jnp.concatenate([left[slot, k, p], right[slot, p, k]], axis=1)
                    for p in range(2)
                    for k in range(col_lines)
                ],
                axis=0,
            )
            for start in range(0, width, tile):
                total[:, start : start + tile] += jnp.dot(
                    gathered,
                    down_buf[j, :, start : start + tile],
                    preferred_element_type=jnp.float32,
                )

        @pl.when((j_now == 1) & (q_now + 1 < NC))
        def _():
            stream_step(q_now + 1)

        @pl.when((j_now == 2) & (q_now + 1 < NC))
        def _():
            norm_step(q_now + 1)

        @pl.when((j_now == 2) & (q_now + 2 < NC))
        def _():
            rs_lines_start(0, q_now + 2)

        @pl.when((j_now == 5) & (q_now + 1 < NC))
        def _():
            ag_forward(q_now + 1)

        @pl.when((i >= steps + 3) & (lax.rem(i - 3, steps) == 0))
        def _():
            q = (i - 4) // steps
            for p in range(2):
                for k in range(col_lines):
                    owner = line(col_lines - k) * 2 + lax.rem(pair_me + p, 2)
                    begin = (p * col_lines + k) * share
                    part[1, q, owner] = (
                        total[begin : begin + share, :].astype(jnp.bfloat16).reshape(2, toks, width)
                    )
            rs_pair(1, q).start()
            total[...] = jnp.zeros_like(total)

        @pl.when((i >= steps + 4) & (lax.rem(i - 4, steps) == 0))
        def _():
            q = (i - 5) // steps
            rs_middle(1, q)
            rs_lines_start(1, q)

        @pl.when((i >= steps + 8) & (lax.rem(i - 8, steps) == 0))
        def _():
            q = (i - 9) // steps
            out_ref[q] = (stream[q] + rs_finish(1, q)).astype(jnp.bfloat16)

        return carry

    lax.fori_loop(0, chunks + 4, iteration, 0)
    rs_middle(1, NC - 1)
    rs_lines_start(1, NC - 1)
    out_ref[NC - 1] = (stream[NC - 1] + rs_finish(1, NC - 1)).astype(jnp.bfloat16)


def tail(attended, out_weight, residual, norm_gain, gate_weight, up_weight, down_weight):
    cols = lax.axis_size("col")
    rows = lax.axis_size("row")
    depth, hidden_width = gate_weight.shape
    tokens, width = residual.shape
    inner = out_weight.shape[0]
    wide = hidden_width // STEPS
    toks = tokens // NC
    share = rows * toks // cols
    col_lines = cols // 2
    row_lines = rows // 2
    assert rows == 2 * cols and inner % wide == 0
    vmem = pl.BlockSpec(memory_space=pltpu.VMEM)
    hbm = pl.BlockSpec(memory_space=pl.ANY)
    dma = pltpu.SemaphoreType.DMA

    def held(*shape):
        return pltpu.VMEM(shape, jnp.bfloat16)

    out = pl.pallas_call(
        functools.partial(tail_kernel, cols, rows),
        out_shape=jax.ShapeDtypeStruct((NC, toks, width), jnp.bfloat16),
        in_specs=[vmem, hbm, vmem, vmem, hbm, hbm, hbm],
        out_specs=vmem,
        scratch_shapes=[
            held(STEPS, depth, wide),
            held(STEPS, depth, wide),
            held(STEPS, wide, width),
            held(NC, cols, 2, toks, inner),
            held(2, NC, row_lines, 2, toks, width),
            held(2, NC, row_lines, toks, width),
            held(2, NC, row_lines, toks, width),
            held(2, NC, row_lines - 1, toks, width),
            pltpu.VMEM((NC, toks, width), jnp.float32),
            pltpu.VMEM((NC, toks, 128), jnp.float32),
            pltpu.VMEM((NC, cols - 1, toks, 128), jnp.float32),
            held(NC, row_lines, 2, toks, depth),
            held(SLOTS, 2, col_lines, share, wide),
            held(SLOTS, col_lines, 2, share, wide),
            held(SLOTS, col_lines, share, wide),
            held(SLOTS, col_lines - 1, 2, share, wide),
            held(SLOTS, col_lines, share, wide),
            held(SLOTS, 2, share, wide),
            held(SLOTS, col_lines - 1, share, wide),
            held(SLOTS, share, wide),
            held(SLOTS, col_lines, 2, share, wide // 2),
            held(SLOTS, 2, col_lines, share, wide // 2),
            pltpu.VMEM((cols * share, width), jnp.float32),
            dma((STEPS,)),
            dma((STEPS,)),
            dma((STEPS,)),
            dma((inner // wide,)),
            dma((NC, cols - 1)),
            dma((NC, cols - 1)),
            dma((2, NC)),
            dma((2, NC)),
            dma((2, NC, row_lines - 1)),
            dma((2, NC, row_lines - 1)),
            dma((NC, cols - 1)),
            dma((NC, cols - 1)),
            dma((NC, row_lines - 1)),
            dma((NC, row_lines - 1)),
            dma((NC, row_lines)),
            dma((NC, row_lines)),
            dma((4, SLOTS)),
            dma((4, SLOTS)),
            dma((4, SLOTS, col_lines - 1)),
            dma((4, SLOTS, col_lines - 1)),
        ],
        compiler_params=pltpu.CompilerParams(
            collective_id=0, has_side_effects=True, vmem_limit_bytes=66 * 1000 * 1000
        ),
    )(
        attended.reshape(2, tokens, inner),
        out_weight,
        residual.reshape(NC, toks, width),
        norm_gain.reshape(1, width),
        gate_weight,
        up_weight,
        down_weight,
    )
    return out.reshape(tokens, width)


def local(
    queries,
    cache_keys,
    cache_values,
    stretch_keys,
    stretch_values,
    block_lists,
    out_weight,
    residual,
    norm_gain,
    gate_weight,
    up_weight,
    down_weight,
):
    row_count = lax.axis_size("row")
    col_count = lax.axis_size("col")
    row_index = lax.axis_index("row")
    col_index = lax.axis_index("col")
    device_count = row_count * col_count
    my_index = row_index * col_count + col_index
    local_blocks = cache_keys.shape[1] // BLK
    heads_here = queries.shape[1] // HEAD_DIM
    list_length = block_lists.shape[2]
    my_group = row_index * heads_here // GROUP
    scaling = 1.0 / math.sqrt(HEAD_DIM)
    targets = jnp.arange(device_count, dtype=jnp.int32)
    target_group = targets // col_count * heads_here // GROUP
    target_lists = block_lists[targets % col_count, target_group]
    holders = target_lists // local_blocks
    matched = holders == my_index
    found_any = jnp.any(matched, axis=1)
    within = jnp.sum(jnp.where(matched, target_lists % local_blocks, 0), axis=1)
    source_rows = target_group * local_blocks + within
    flat_keys = cache_keys.reshape(KV_HEADS * local_blocks, BLK, HEAD_DIM)
    flat_values = cache_values.reshape(KV_HEADS * local_blocks, BLK, HEAD_DIM)
    outgoing = jnp.concatenate([flat_keys[source_rows], flat_values[source_rows]], axis=2)
    outgoing = jnp.where(found_any[:, None, None], outgoing, jnp.zeros_like(outgoing))
    arrived = lax.all_to_all(outgoing, ("row", "col"), split_axis=0, concat_axis=0, tiled=True)
    my_list = block_lists[col_index, my_group]
    fetched = arrived[my_list // local_blocks].reshape(list_length * BLK, 2 * HEAD_DIM)
    far_keys = fetched[:, :HEAD_DIM]
    far_values = fetched[:, HEAD_DIM:]
    query_rows = queries.reshape(BLK * heads_here, HEAD_DIM)
    far_scores = jnp.dot(query_rows, far_keys.T, preferred_element_type=jnp.float32) * scaling
    run_max = jnp.max(far_scores, axis=1)
    far_exp = jnp.exp(far_scores - run_max[:, None])
    run_sum = jnp.sum(far_exp, axis=1)
    run_acc = jnp.dot(far_exp.astype(jnp.bfloat16), far_values, preferred_element_type=jnp.float32)
    query_pos = col_index * BLK + jnp.arange(BLK * heads_here, dtype=jnp.int32) // heads_here
    own = jnp.concatenate([stretch_keys, stretch_values], axis=2)
    own = lax.dynamic_index_in_dim(own, my_group, 0, keepdims=False)
    piece = lax.all_gather(own, "col", axis=0, tiled=True)
    piece_keys = piece[:, :HEAD_DIM]
    piece_values = piece[:, HEAD_DIM:]
    scores = jnp.dot(query_rows, piece_keys.T, preferred_element_type=jnp.float32) * scaling
    key_pos = jnp.arange(piece_keys.shape[0], dtype=jnp.int32)
    allowed = key_pos[None, :] <= query_pos[:, None]
    scores = jnp.where(allowed, scores, -1e30)
    new_max = jnp.maximum(run_max, jnp.max(scores, axis=1))
    decays = jnp.exp(run_max - new_max)
    weights = jnp.where(allowed, jnp.exp(scores - new_max[:, None]), 0.0)
    new_sum = run_sum * decays + jnp.sum(weights, axis=1)
    new_acc = run_acc * decays[:, None] + jnp.dot(
        weights.astype(jnp.bfloat16), piece_values, preferred_element_type=jnp.float32
    )
    attended = (new_acc / new_sum[:, None]).astype(jnp.bfloat16).reshape(BLK, heads_here * HEAD_DIM)
    return tail(attended, out_weight, residual, norm_gain, gate_weight, up_weight, down_weight)


def solution(mesh):
    in_specs = (
        P("col", "row"),
        P(None, ("row", "col"), None),
        P(None, ("row", "col"), None),
        P(None, "col", None),
        P(None, "col", None),
        P(),
        P("row", "col"),
        P("row", "col"),
        P("col"),
        P("col", "row"),
        P("col", "row"),
        P("row", "col"),
    )
    out_specs = P("row", "col")
    return jax.shard_map(local, mesh=mesh, in_specs=in_specs, out_specs=out_specs, check_vma=False)
```

time: 289 us -> 221 us (0.76)
  waiting for transfers between devices: 55.7 us -> 24.8 us
  Pallas kernels: 169 us -> 147 us
  between operations: 13.7 us -> 0.19 us
    all_gather x1 -> x0, waiting for transfers between devices: 30.9 us -> none  [local(): pieces = lax.all_gather(outgoing_piece, 'row', axis=0, tiled=True)]
    pallas_call x4 -> x1, Pallas kernels: 169 us -> 147 us  [tail(): pl.pallas_call(functools.partial(tail_kernel, cols, rows), out_shape=jax....]
  transfers between devices with their start and end apart: 2 -> 1, of which waited for: 2 -> 1; matrix products, arithmetic and copies ran while one was open for 1% -> 1% of each run, Pallas kernels for 0% -> 0%
where the time goes in v1:
time: 221 us; the launch traced here: 220 us
  Pallas kernels  147 us (67%)
  waiting for transfers between devices  24.8 us (11%)
  blocking collectives  20.6 us (9%)
  local copies, waits for them, and re-layouts  10 us (5%)
  starting transfers between devices  7.33 us (3%)
  matrix products  5.3 us (2%)
  other arithmetic  5.13 us (2%)
    pallas_call x1, Pallas kernels, tail(): pl.pallas_call(functools.partial(tail_kernel, cols, rows), out_shape=jax....  147 us
    all_to_all x1, waiting for transfers between devices, local(): lax.all_to_all(outgoing, ('row', 'col'), split_axis=0, concat_axis=0, til...  24.8 us
    all_gather x1, blocking collectives, local(): piece = lax.all_gather(own, 'col', axis=0, tiled=True)  20.6 us
    all_to_all x1, starting transfers between devices, local(): lax.all_to_all(outgoing, ('row', 'col'), split_axis=0, concat_axis=0, til...  7.33 us
  transfers between devices with their start and end apart: 1, of which 1 were waited for; matrix products, arithmetic and copies ran while one was open for 1% of the time, Pallas kernels for 0%

profile of v1, /device:TPU:0, one launch (start us, length us, event | category | flops | bytes accessed | tf_op | source)
XLA Modules:
  0.0 220.5 jit_solution(6470732462713918956)
XLA Ops:
  0.0 1.4 gather_fusion
  1.4 0.1 fusion.48
  1.5 0.1 fusion.27
  1.7 2.3 %gather_fusion.1 = bf16[32,128,128]{2,1,0:T(8,128)(2,1)S(1)} fusion(bf16[64,128,128]{2,1,0:T(8,128)(2,1)} %bitcast.38, s32[1024]{0:T(1024)S(1)} %pad_clamp_fusion.1), kind=kCustom, calls=%fused_computation.1 | custom fusion | bytes 2097280 | tf_op jit(solution)/shard_map/gather | solution.py:583
  4.0 2.3 %gather_fusion.2 = bf16[32,128,128]{2,1,0:T(8,128)(2,1)S(1)} fusion(bf16[64,128,128]{2,1,0:T(8,128)(2,1)} %bitcast.39, s32[1024]{0:T(1024)S(1)} %pad_clamp_fusion.1), kind=kCustom, calls=%fused_computation.2 | custom fusion | bytes 2097280 | tf_op jit(solution)/shard_map/gather | solution.py:583
  6.4 2.1 maximum_select_fusion
  8.5 0.0 copy-start.3
  8.5 0.0 copy-start.6
  8.5 0.0 copy-start.4
  8.5 0.0 copy-start.5
  8.5 7.3 %all-to-all-start = ((bf16[32,128,256]{2,1,0:T(8,128)(2,1)}), bf16[32,128,256]{2,1,0:T(8,128)(2,1)S(1)}, u32[]{:S(2)}, u32[]{:S(2)}) async-start(bf16[32,128,256]{2,1,0:T(8,128)(2,1)} %maximum_select_fusion), calls=%async_computation | async-start | bytes 4194304 | tf_op jit(solution)/shard_map/all_to_all | solution.py:585
  15.8 0.0 copy-done.3
  15.8 0.1 reshape.276
  16.0 0.0 copy-done.6
  16.0 0.6 reshape.278.gain_ref
  16.6 0.0 copy-done.4
  16.6 0.0 copy-done.5
  16.6 20.6 %all-gather = bf16[1,512,256]{2,1,0:T(8,128)(2,1)S(1)} all-gather(bf16[1,128,256]{2,1,0:T(8,128)(2,1)S(1)} %fusion.24), channel_id=2, replica_groups=mesh['row'=8,'col'=4] {'col'}, dimensions={1}, use_global_device_ids=true | all-gather | bytes 327680 | tf_op jit(solution)/shard_map/all_gather | solution.py:599
  37.2 0.0 copy-start.1
  37.2 0.7 fusion.42
  37.9 0.0 copy-done.1
  37.9 1.8 fusion.4
  39.7 24.8 %all-to-all-done = bf16[32,128,256]{2,1,0:T(8,128)(2,1)S(1)} async-done(((bf16[32,128,256]{2,1,0:T(8,128)(2,1)}), bf16[32,128,256]{2,1,0:T(8,128)(2,1)S(1)}, u32[]{:S(2)}, u32[]{:S(2)}) %all-to-all-start) | async-done | bytes 2097184 | tf_op jit(solution)/shard_map/all_to_all | solution.py:585
  64.5 0.6 gather_fusion.3
  65.1 1.3 multiply_reduce_fusion
  66.4 0.0 copy-start
  66.4 1.4 fusion
  67.8 0.1 copy-done
  68.0 0.6 fusion.6
  68.6 0.0 copy-start.2
  68.6 1.5 fusion.8
  70.1 0.0 copy-done.2
  70.1 0.8 fusion.11
  70.9 0.8 reshape_reshape.3.att_ref
  71.7 147.1 %shard_map.118 = bf16[4,16,2048]{2,1,0:T(8,128)(2,1)} custom-call(bf16[2,64,1024]{2,1,0:T(8,128)(2,1)} %reshape_reshape.3.att_ref, bf16[1024,2048]{1,0:T(8,128)(2,1)} %wo_ref.1, bf16[4,16,2048]{2,1,0:T(8,128)(2,1)} %bitcast.40, bf16[1,2048]{1,0:T(2,128)(2,1)} %reshape.278.gain_ref, bf16[2048,3584]{1,0:T(8,128)(2,1)} %gate_ref.1, bf16[2048,3584]{1,0:T(8,128)(2,1)} %up_ref.1, ...), custom_call_target="tpu_custom_call" | custom-call | tf_op jit(solution)/shard_map/pallas_call | solution.py:483
  218.8 1.7 copy.14
  (8 shorter events, 0.1 us)
Async XLA Ops:
  8.5 7.4 %copy-start.3 = (bf16[128,1024]{1,0:T(8,128)(2,1)S(1)}, bf16[128,1024]{1,0:T(8,128)(2,1)}, u32[]{:S(2)}) copy-start(bf16[128,1024]{1,0:T(8,128)(2,1)} %param.12) | copy-start | bytes 786436
  8.5 7.5 %copy-start.6 = (bf16[2048]{0:T(1024)(128)(2,1)S(1)}, bf16[2048]{0:T(1024)(128)(2,1)}, u32[]{:S(2)}) copy-start(bf16[2048]{0:T(1024)(128)(2,1)} %param.20) | copy-start | bytes 12292
  8.5 8.1 %copy-start.4 = (bf16[8,128,128]{2,1,0:T(8,128)(2,1)S(1)}, bf16[8,128,128]{2,1,0:T(8,128)(2,1)}, u32[]{:S(2)}) copy-start(bf16[8,128,128]{2,1,0:T(8,128)(2,1)} %param.15) | copy-start | bytes 786436
  8.5 8.1 %copy-start.5 = (bf16[8,128,128]{2,1,0:T(8,128)(2,1)S(1)}, bf16[8,128,128]{2,1,0:T(8,128)(2,1)}, u32[]{:S(2)}) copy-start(bf16[8,128,128]{2,1,0:T(8,128)(2,1)} %param.16) | copy-start | bytes 786436
  8.5 56.0 %all-to-all-start = ((bf16[32,128,256]{2,1,0:T(8,128)(2,1)}), bf16[32,128,256]{2,1,0:T(8,128)(2,1)S(1)}, u32[]{:S(2)}, u32[]{:S(2)}) async-start(bf16[32,128,256]{2,1,0:T(8,128)(2,1)} %maximum_select_fusion), calls=%async_computation | async-start | bytes 4194304 | tf_op jit(solution)/shard_map/all_to_all | solution.py:585
  37.2 0.7 copy-start.1
  66.4 1.6 copy-start
  68.6 1.5 copy-start.2

commit v2 on v1

--- a/solution.py
+++ b/solution.py
@@ -16,6 +16,231 @@
 MESH = pl.DeviceIdType.MESH
 NC = 4
 STEPS = 7
+
+
+def gather_kernel(devices, rows_ref, keys_ref, values_ref, out_ref, key_sem, value_sem):
+    groups = keys_ref.shape[0]
+
+    def copies(d):
+        group = d * groups // devices
+        positions = pl.ds(pl.multiple_of(rows_ref[d] * BLK, BLK), BLK)
+        return (
+            pltpu.make_async_copy(keys_ref.at[group, positions], out_ref.at[d, 0], key_sem.at[d]),
+            pltpu.make_async_copy(values_ref.at[group, positions], out_ref.at[d, 1], value_sem.at[d]),
+        )
+
+    for d in range(devices):
+        for copy in copies(d):
+            copy.start()
+    for d in range(devices):
+        for copy in copies(d):
+            copy.wait()
+
+
+def gather_blocks(block_rows, cache_keys, cache_values):
+    devices = block_rows.shape[0]
+    dma = pltpu.SemaphoreType.DMA
+    return pl.pallas_call(
+        functools.partial(gather_kernel, devices),
+        out_shape=jax.ShapeDtypeStruct((devices, 2, BLK, HEAD_DIM), cache_keys.dtype),
+        in_specs=[
+            pl.BlockSpec(memory_space=pltpu.SMEM),
+            pl.BlockSpec(memory_space=pl.ANY),
+            pl.BlockSpec(memory_space=pl.ANY),
+        ],
+        out_specs=pl.BlockSpec(memory_space=pltpu.VMEM),
+        scratch_shapes=[dma((devices,)), dma((devices,))],
+        compiler_params=pltpu.CompilerParams(vmem_limit_bytes=16 * 1024 * 1024),
+    )(block_rows, cache_keys, cache_values)
+
+
+def flipped(index, bits):
+    result = index
+    place = 1
+    while place <= bits:
+        if bits // place % 2:
+            result = result + place * (1 - 2 * lax.rem(index // place, 2))
+        place *= 2
+    return result
+
+
+def attend_kernel(
+    rows,
+    cols,
+    query_ref,
+    block_ref,
+    bias_ref,
+    near_key_ref,
+    near_value_ref,
+    out_ref,
+    held,
+    near,
+    heads_first,
+    top,
+    norm,
+    acc,
+    near_sem,
+    near_send,
+    near_recv,
+    block_send,
+    block_recv,
+):
+    row = lax.axis_index("row")
+    col = lax.axis_index("col")
+    devices = rows * cols
+    heads = query_ref.shape[1] // HEAD_DIM
+    group = row * heads // GROUP
+    scaling = 1.0 / math.sqrt(HEAD_DIM)
+    pairs = heads // 2
+    order = sorted(range(devices), key=lambda k: (k // cols // 2, k))
+    slot_of = {k: s for s, k in enumerate(order)}
+
+    def peer(k):
+        return flipped(row, k // cols), flipped(col, k % cols)
+
+    def block_copy(k):
+        peer_row, peer_col = peer(k)
+        slot = slot_of[k]
+        return pltpu.make_async_remote_copy(
+            src_ref=block_ref.at[peer_row * cols + peer_col],
+            dst_ref=held.at[slot],
+            send_sem=block_send.at[slot],
+            recv_sem=block_recv.at[slot],
+            device_id={"row": peer_row, "col": peer_col},
+            device_id_type=MESH,
+        )
+
+    def near_copy(k):
+        return pltpu.make_async_remote_copy(
+            src_ref=near.at[col],
+            dst_ref=near.at[col],
+            send_sem=near_send.at[k - 1],
+            recv_sem=near_recv.at[k - 1],
+            device_id={"col": flipped(col, k)},
+            device_id_type=MESH,
+        )
+
+    own = (
+        pltpu.make_async_copy(near_key_ref.at[group], near.at[col, 0], near_sem.at[0]),
+        pltpu.make_async_copy(near_value_ref.at[group], near.at[col, 1], near_sem.at[1]),
+    )
+    for copy in own:
+        copy.start()
+    barrier = pltpu.get_barrier_semaphore()
+    for k in range(1, devices):
+        peer_row, peer_col = peer(k)
+        pl.semaphore_signal(
+            barrier, inc=1, device_id={"row": peer_row, "col": peer_col}, device_id_type=MESH
+        )
+    pl.semaphore_wait(barrier, devices - 1)
+    for copy in own:
+        copy.wait()
+    for k in range(1, cols):
+        near_copy(k).start()
+    for k in sorted(range(1, devices), key=lambda k: (-(k // cols // 2), k)):
+        block_copy(k).start()
+    held[0] = block_ref[row * cols + col]
+    for h in range(heads):
+        heads_first[h * BLK : (h + 1) * BLK, :] = query_ref[:, h * HEAD_DIM : (h + 1) * HEAD_DIM]
+    for k in range(1, cols):
+        near_copy(k).wait()
+
+    def near_pass(p, carry):
+        lines = pl.ds(pl.multiple_of(p * 2 * BLK, 2 * BLK), 2 * BLK)
+        keys = near[:, 0].reshape(cols * BLK, HEAD_DIM)
+        scores = lax.dot_general(
+            heads_first[lines, :], keys, (((1,), (1,)), ((), ())), preferred_element_type=jnp.float32
+        ) * scaling
+        position = lax.broadcasted_iota(jnp.int32, scores.shape, 1)
+        token = col * BLK + lax.rem(lax.broadcasted_iota(jnp.int32, scores.shape, 0), BLK)
+        allowed = position <= token
+        scores = jnp.where(allowed, scores, -1e30)
+        new_top = jnp.max(scores, axis=1, keepdims=True)
+        weights = jnp.where(allowed, jnp.exp(scores - new_top), 0.0)
+        top[lines, :] = jnp.broadcast_to(new_top, (2 * BLK, HEAD_DIM))
+        norm[lines, :] = jnp.broadcast_to(jnp.sum(weights, axis=1, keepdims=True), (2 * BLK, HEAD_DIM))
+        acc[lines, :] = jnp.dot(
+            weights.astype(jnp.bfloat16),
+            near[:, 1].reshape(cols * BLK, HEAD_DIM),
+            preferred_element_type=jnp.float32,
+        )
+        return carry
+
+    lax.fori_loop(0, pairs, near_pass, 0)
+
+    batch = 4
+    for first in range(0, devices, batch):
+        bias = []
+        for slot in range(first, first + batch):
+            k = order[slot]
+            if k:
+                block_copy(k).wait()
+            peer_row, peer_col = peer(k)
+            bias.append(bias_ref[peer_row * cols + peer_col])
+        bias = jnp.concatenate(bias, axis=1)
+
+        def far_pass(p, carry):
+            lines = pl.ds(pl.multiple_of(p * 2 * BLK, 2 * BLK), 2 * BLK)
+            keys = held[first : first + batch, 0].reshape(batch * BLK, HEAD_DIM)
+            scores = (
+                lax.dot_general(
+                    heads_first[lines, :], keys, (((1,), (1,)), ((), ())), preferred_element_type=jnp.float32
+                )
+                * scaling
+                + bias
+            )
+            old_top = top[lines, :]
+            new_top = jnp.maximum(old_top, jnp.max(scores, axis=1, keepdims=True))
+            decay = jnp.exp(old_top - new_top)
+            weights = jnp.exp(scores - new_top[:, :1])
+            top[lines, :] = new_top
+            norm[lines, :] = norm[lines, :] * decay + jnp.sum(weights, axis=1, keepdims=True)
+            acc[lines, :] = acc[lines, :] * decay + jnp.dot(
+                weights.astype(jnp.bfloat16),
+                held[first : first + batch, 1].reshape(batch * BLK, HEAD_DIM),
+                preferred_element_type=jnp.float32,
+            )
+            return carry
+
+        lax.fori_loop(0, pairs, far_pass, 0)
+    halves = out_ref.shape[1]
+    for h in range(heads):
+        lines = slice(h * BLK, (h + 1) * BLK)
+        result = (acc[lines, :] / norm[lines, :]).astype(jnp.bfloat16)
+        for p in range(BLK // halves):
+            out_ref[p, :, h * HEAD_DIM : (h + 1) * HEAD_DIM] = result[p * halves : (p + 1) * halves]
+
+
+def attend(queries, blocks, bias, stretch_keys, stretch_values, tokens):
+    rows = lax.axis_size("row")
+    cols = lax.axis_size("col")
+    devices = rows * cols
+    lines = BLK * queries.shape[1] // HEAD_DIM
+    vmem = pl.BlockSpec(memory_space=pltpu.VMEM)
+    hbm = pl.BlockSpec(memory_space=pl.ANY)
+    dma = pltpu.SemaphoreType.DMA
+    return pl.pallas_call(
+        functools.partial(attend_kernel, rows, cols),
+        out_shape=jax.ShapeDtypeStruct((BLK // tokens, tokens, queries.shape[1]), jnp.bfloat16),
+        in_specs=[vmem, vmem, vmem, hbm, hbm],
+        out_specs=vmem,
+        scratch_shapes=[
+            pltpu.VMEM((devices, 2, BLK, HEAD_DIM), jnp.bfloat16),
+            pltpu.VMEM((cols, 2, BLK, HEAD_DIM), jnp.bfloat16),
+            pltpu.VMEM((lines, HEAD_DIM), jnp.bfloat16),
+            pltpu.VMEM((lines, HEAD_DIM), jnp.float32),
+            pltpu.VMEM((lines, HEAD_DIM), jnp.float32),
+            pltpu.VMEM((lines, HEAD_DIM), jnp.float32),
+            dma((2,)),
+            dma((cols - 1,)),
+            dma((cols - 1,)),
+            dma((devices,)),
+            dma((devices,)),
+        ],
+        compiler_params=pltpu.CompilerParams(
+            collective_id=1, has_side_effects=True, vmem_limit_bytes=40 * 1024 * 1024
+        ),
+    )(queries, blocks, bias, stretch_keys, stretch_values)
 
 
 def tail_kernel(
@@ -451,14 +676,14 @@
         @pl.when((i >= steps + 8) & (lax.rem(i - 8, steps) == 0))
         def _():
             q = (i - 9) // steps
-            out_ref[q] = (stream[q] + rs_finish(1, q)).astype(jnp.bfloat16)
+            out_ref[q] = stream[q] + rs_finish(1, q)
 
         return carry
 
     lax.fori_loop(0, chunks + 4, iteration, 0)
     rs_middle(1, NC - 1)
     rs_lines_start(1, NC - 1)
-    out_ref[NC - 1] = (stream[NC - 1] + rs_finish(1, NC - 1)).astype(jnp.bfloat16)
+    out_ref[NC - 1] = stream[NC - 1] + rs_finish(1, NC - 1)
 
 
 def tail(attended, out_weight, residual, norm_gain, gate_weight, up_weight, down_weight):
@@ -482,7 +707,7 @@
 
     out = pl.pallas_call(
         functools.partial(tail_kernel, cols, rows),
-        out_shape=jax.ShapeDtypeStruct((NC, toks, width), jnp.bfloat16),
+        out_shape=jax.ShapeDtypeStruct((NC, toks, width), jnp.float32),
         in_specs=[vmem, hbm, vmem, vmem, hbm, hbm, hbm],
         out_specs=vmem,
         scratch_shapes=[
@@ -534,7 +759,7 @@
             collective_id=0, has_side_effects=True, vmem_limit_bytes=66 * 1000 * 1000
         ),
     )(
-        attended.reshape(2, tokens, inner),
+        attended,
         out_weight,
         residual.reshape(NC, toks, width),
         norm_gain.reshape(1, width),
@@ -542,7 +767,7 @@
         up_weight,
         down_weight,
     )
-    return out.reshape(tokens, width)
+    return out.reshape(tokens, width).astype(jnp.bfloat16)
 
 
 def local(
@@ -567,50 +792,16 @@
     my_index = row_index * col_count + col_index
     local_blocks = cache_keys.shape[1] // BLK
     heads_here = queries.shape[1] // HEAD_DIM
-    list_length = block_lists.shape[2]
-    my_group = row_index * heads_here // GROUP
-    scaling = 1.0 / math.sqrt(HEAD_DIM)
-    targets = jnp.arange(device_count, dtype=jnp.int32)
-    target_group = targets // col_count * heads_here // GROUP
-    target_lists = block_lists[targets % col_count, target_group]
-    holders = target_lists // local_blocks
-    matched = holders == my_index
-    found_any = jnp.any(matched, axis=1)
-    within = jnp.sum(jnp.where(matched, target_lists % local_blocks, 0), axis=1)
-    source_rows = target_group * local_blocks + within
-    flat_keys = cache_keys.reshape(KV_HEADS * local_blocks, BLK, HEAD_DIM)
-    flat_values = cache_values.reshape(KV_HEADS * local_blocks, BLK, HEAD_DIM)
-    outgoing = jnp.concatenate([flat_keys[source_rows], flat_values[source_rows]], axis=2)
-    outgoing = jnp.where(found_any[:, None, None], outgoing, jnp.zeros_like(outgoing))
-    arrived = lax.all_to_all(outgoing, ("row", "col"), split_axis=0, concat_axis=0, tiled=True)
-    my_list = block_lists[col_index, my_group]
-    fetched = arrived[my_list // local_blocks].reshape(list_length * BLK, 2 * HEAD_DIM)
-    far_keys = fetched[:, :HEAD_DIM]
-    far_values = fetched[:, HEAD_DIM:]
-    query_rows = queries.reshape(BLK * heads_here, HEAD_DIM)
-    far_scores = jnp.dot(query_rows, far_keys.T, preferred_element_type=jnp.float32) * scaling
-    run_max = jnp.max(far_scores, axis=1)
-    far_exp = jnp.exp(far_scores - run_max[:, None])
-    run_sum = jnp.sum(far_exp, axis=1)
-    run_acc = jnp.dot(far_exp.astype(jnp.bfloat16), far_values, preferred_element_type=jnp.float32)
-    query_pos = col_index * BLK + jnp.arange(BLK * heads_here, dtype=jnp.int32) // heads_here
-    own = jnp.concatenate([stretch_keys, stretch_values], axis=2)
-    own = lax.dynamic_index_in_dim(own, my_group, 0, keepdims=False)
-    piece = lax.all_gather(own, "col", axis=0, tiled=True)
-    piece_keys = piece[:, :HEAD_DIM]
-    piece_values = piece[:, HEAD_DIM:]
-    scores = jnp.dot(query_rows, piece_keys.T, preferred_element_type=jnp.float32) * scaling
-    key_pos = jnp.arange(piece_keys.shape[0], dtype=jnp.int32)
-    allowed = key_pos[None, :] <= query_pos[:, None]
-    scores = jnp.where(allowed, scores, -1e30)
-    new_max = jnp.maximum(run_max, jnp.max(scores, axis=1))
-    decays = jnp.exp(run_max - new_max)
-    weights = jnp.where(allowed, jnp.exp(scores - new_max[:, None]), 0.0)
-    new_sum = run_sum * decays + jnp.sum(weights, axis=1)
-    new_acc = run_acc * decays[:, None] + jnp.dot(
-        weights.astype(jnp.bfloat16), piece_values, preferred_element_type=jnp.float32
-    )
-    attended = (new_acc / new_sum[:, None]).astype(jnp.bfloat16).reshape(BLK, heads_here * HEAD_DIM)
+    lists = jnp.swapaxes(block_lists, 0, 1)
+    lists = jnp.repeat(lists, row_count // KV_HEADS, axis=0).reshape(device_count, -1)
+    matched = lists // local_blocks == my_index
+    block_rows = jnp.sum(jnp.where(matched, lists % local_blocks, 0), axis=1)
+    blocks = gather_blocks(block_rows, cache_keys, cache_values)
+    my_list = block_lists[col_index, row_index * heads_here // GROUP]
+    sources = jnp.arange(device_count, dtype=jnp.int32)
+    wanted = jnp.any(my_list[None, :] // local_blocks == sources[:, None], axis=1)
+    bias = jnp.broadcast_to(jnp.where(wanted, 0.0, -1e30)[:, None, None], (device_count, 1, BLK))
+    attended = attend(queries, blocks, bias, stretch_keys, stretch_values, residual.shape[0])
     return tail(attended, out_weight, residual, norm_gain, gate_weight, up_weight, down_weight)
 
 

time: 221 us -> 222 us (level)
  Pallas kernels: 147 us -> 214 us
  waiting for transfers between devices: 24.8 us -> 0 us
  blocking collectives: 20.6 us -> 0 us
  starting transfers between devices: 7.33 us -> 0 us
  matrix products: 5.3 us -> 0 us
  local copies, waits for them, and re-layouts: 10 us -> 4.76 us
    pallas_call x0 -> x2, Pallas kernels: none -> 66.3 us  [the longest x1 62.2 us: attend(): pl.pallas_call(functools.partial(attend_kernel, rows, cols), out_shape=ja...]
    all_to_all x1 -> x0, waiting for transfers between devices: 24.8 us -> none  [local(): lax.all_to_all(outgoing, ('row', 'col'), split_axis=0, concat_axis=0, til...]
    all_gather x1 -> x0, blocking collectives: 20.6 us -> none  [local(): piece = lax.all_gather(own, 'col', axis=0, tiled=True)]
    all_to_all x1 -> x0, starting transfers between devices: 7.33 us -> none  [local(): lax.all_to_all(outgoing, ('row', 'col'), split_axis=0, concat_axis=0, til...]
    gather x4 -> x0, local copies, waits for them, and re-layouts: 6.67 us -> none  [the longest x1 2.34 us: local(): flat_values[source_rows]]
    dot_general x4 -> x0, matrix products: 5.3 us -> none  [the longest x1 1.77 us: local(): jnp.dot(query_rows, piece_keys.T, preferred_element_type=jnp.float32)]
  transfers between devices with their start and end apart: 1 -> 0, of which waited for: 1 -> 0; matrix products, arithmetic and copies ran while one was open for 1% -> 0% of each run, Pallas kernels for 0% -> 0%
where the time goes in v2:
time: 222 us
  Pallas kernels  214 us (96%)
  local copies, waits for them, and re-layouts  4.76 us (2%)
  other arithmetic  3.44 us (2%)
    pallas_call x1, Pallas kernels, tail(): pl.pallas_call(functools.partial(tail_kernel, cols, rows), out_shape=jax....  148 us
    pallas_call x1, Pallas kernels, attend(): pl.pallas_call(functools.partial(attend_kernel, rows, cols), out_shape=ja...  62.2 us

profile of v2, /device:TPU:0, one launch (start us, length us, event | category | flops | bytes accessed | tf_op | source)
XLA Modules:
  0.0 222.1 jit_solution(2270563937052388521)
XLA Ops:
  0.0 0.7 and_select_fusion
  0.7 0.1 fusion.6
  0.8 0.1 broadcast_in_dim.19.bias_ref
  0.9 0.9 fusion.2
  1.8 0.1 copy.14
  1.9 0.1 reduce_sum.12.rows_ref
  1.9 0.0 copy-start
  1.9 1.6 copy-done
  3.5 0.0 copy-start.1
  3.5 1.6 copy-done.1
  5.1 0.0 copy-start.3
  5.1 0.0 copy-start.4
  5.1 0.0 copy-start.5
  5.1 0.0 copy-start.6
  5.1 4.1 %shard_map.118.block_ref = bf16[32,2,128,128]{3,2,1,0:T(8,128)(2,1)S(1)} custom-call(s32[32]{0:T(128)S(1)} %reduce_sum.12.rows_ref, bf16[8,1024,128]{2,1,0:T(8,128)(2,1)S(1)} %copy-done, bf16[8,1024,128]{2,1,0:T(8,128)(2,1)S(1)} %copy-done.1), custom_call_target="tpu_custom_call" | custom-call | tf_op jit(solution)/shard_map/pallas_call | solution.py:43
  9.3 0.0 copy-done.3
  9.3 0.0 copy-done.4
  9.3 0.0 copy-done.5
  9.3 62.2 %shard_map.119.att_ref = bf16[2,64,1024]{2,1,0:T(8,128)(2,1)S(1)} custom-call(bf16[128,1024]{1,0:T(8,128)(2,1)S(1)} %copy-done.3, bf16[32,2,128,128]{3,2,1,0:T(8,128)(2,1)S(1)} %shard_map.118.block_ref, f32[32,1,128]{2,1,0:T(1,128)S(1)} %broadcast_in_dim.19.bias_ref, bf16[8,128,128]{2,1,0:T(8,128)(2,1)S(1)} %copy-done.4, bf16[8,128,128]{2,1,0:T(8,128)(2,1)S(1)} %copy-done.5), custom_call_target="tpu_custom_call" | custom-call | tf_op jit(solution)/shard_map/pallas_call | solution.py:222
  71.5 0.0 copy-start.2
  71.5 0.7 copy-done.2
  72.2 0.0 copy-done.6
  72.2 0.6 reshape.74.gain_ref
  72.8 147.5 %shard_map.120 = f32[4,16,2048]{2,1,0:T(8,128)} custom-call(bf16[2,64,1024]{2,1,0:T(8,128)(2,1)} %copy-done.2, bf16[1024,2048]{1,0:T(8,128)(2,1)} %wo_ref.1, bf16[4,16,2048]{2,1,0:T(8,128)(2,1)} %bitcast.28, bf16[1,2048]{1,0:T(2,128)(2,1)} %reshape.74.gain_ref, bf16[2048,3584]{1,0:T(8,128)(2,1)} %gate_ref.1, bf16[2048,3584]{1,0:T(8,128)(2,1)} %up_ref.1, ...), custom_call_target="tpu_custom_call" | custom-call | tf_op jit(solution)/shard_map/pallas_call | solution.py:708
  220.3 1.8 convert_element_type.6
  (1 shorter events, 0.0 us)
Async XLA Ops:
  1.9 1.6 copy-start
  3.5 1.6 copy-start.1
  5.1 4.1 %copy-start.3 = (bf16[128,1024]{1,0:T(8,128)(2,1)S(1)}, bf16[128,1024]{1,0:T(8,128)(2,1)}, u32[]{:S(2)}) copy-start(bf16[128,1024]{1,0:T(8,128)(2,1)} %query_ref.1) | copy-start | bytes 786436
  5.1 4.1 %copy-start.4 = (bf16[8,128,128]{2,1,0:T(8,128)(2,1)S(1)}, bf16[8,128,128]{2,1,0:T(8,128)(2,1)}, u32[]{:S(2)}) copy-start(bf16[8,128,128]{2,1,0:T(8,128)(2,1)} %near_key_ref.1) | copy-start | bytes 786436
  5.1 4.1 %copy-start.5 = (bf16[8,128,128]{2,1,0:T(8,128)(2,1)S(1)}, bf16[8,128,128]{2,1,0:T(8,128)(2,1)}, u32[]{:S(2)}) copy-start(bf16[8,128,128]{2,1,0:T(8,128)(2,1)} %near_value_ref.1) | copy-start | bytes 786436
  5.1 67.0 %copy-start.6 = (bf16[2048]{0:T(1024)(128)(2,1)S(1)}, bf16[2048]{0:T(1024)(128)(2,1)}, u32[]{:S(2)}) copy-start(bf16[2048]{0:T(1024)(128)(2,1)} %param.20) | copy-start | bytes 12292
  71.5 0.7 copy-start.2

commit v3 on v2

--- a/solution.py
+++ b/solution.py
@@ -12,18 +12,22 @@
 HEAD_DIM = 128
 BLK = 128
 GROUP = 8
-SLOTS = 4
+SLOTS = 8
+HOLD = 4
+LAGS = (0, 2, 4, 6, 8)
 MESH = pl.DeviceIdType.MESH
 NC = 4
 STEPS = 7
 
 
-def gather_kernel(devices, rows_ref, keys_ref, values_ref, out_ref, key_sem, value_sem):
+def gather_kernel(rows_ref, keys_ref, values_ref, out_ref, key_sem, value_sem):
     groups = keys_ref.shape[0]
+    cols = rows_ref.shape[0]
+    devices = out_ref.shape[0]
 
     def copies(d):
         group = d * groups // devices
-        positions = pl.ds(pl.multiple_of(rows_ref[d] * BLK, BLK), BLK)
+        positions = pl.ds(pl.multiple_of(rows_ref[d % cols, group] * BLK, BLK), BLK)
         return (
             pltpu.make_async_copy(keys_ref.at[group, positions], out_ref.at[d, 0], key_sem.at[d]),
             pltpu.make_async_copy(values_ref.at[group, positions], out_ref.at[d, 1], value_sem.at[d]),
@@ -37,11 +41,10 @@
             copy.wait()
 
 
-def gather_blocks(block_rows, cache_keys, cache_values):
-    devices = block_rows.shape[0]
+def gather_blocks(block_rows, cache_keys, cache_values, devices):
     dma = pltpu.SemaphoreType.DMA
     return pl.pallas_call(
-        functools.partial(gather_kernel, devices),
+        gather_kernel,
         out_shape=jax.ShapeDtypeStruct((devices, 2, BLK, HEAD_DIM), cache_keys.dtype),
         in_specs=[
             pl.BlockSpec(memory_space=pltpu.SMEM),
@@ -50,7 +53,7 @@
         ],
         out_specs=pl.BlockSpec(memory_space=pltpu.VMEM),
         scratch_shapes=[dma((devices,)), dma((devices,))],
-        compiler_params=pltpu.CompilerParams(vmem_limit_bytes=16 * 1024 * 1024),
+        compiler_params=pltpu.CompilerParams(vmem_limit_bytes=63 * 1024 * 1024),
     )(block_rows, cache_keys, cache_values)
 
 
@@ -64,12 +67,14 @@
     return result
 
 
-def attend_kernel(
+def attention(
     rows,
     cols,
+    local_blocks,
+    begin,
     query_ref,
     block_ref,
-    bias_ref,
+    lists_ref,
     near_key_ref,
     near_value_ref,
     out_ref,
@@ -124,8 +129,10 @@
         pltpu.make_async_copy(near_key_ref.at[group], near.at[col, 0], near_sem.at[0]),
         pltpu.make_async_copy(near_value_ref.at[group], near.at[col, 1], near_sem.at[1]),
     )
+    own_block = pltpu.make_async_copy(block_ref.at[row * cols + col], held.at[0], near_sem.at[2])
     for copy in own:
         copy.start()
+    own_block.start()
     barrier = pltpu.get_barrier_semaphore()
     for k in range(1, devices):
         peer_row, peer_col = peer(k)
@@ -137,9 +144,9 @@
         copy.wait()
     for k in range(1, cols):
         near_copy(k).start()
-    for k in sorted(range(1, devices), key=lambda k: (-(k // cols // 2), k)):
+    for k in order[1:]:
         block_copy(k).start()
-    held[0] = block_ref[row * cols + col]
+    begin()
     for h in range(heads):
         heads_first[h * BLK : (h + 1) * BLK, :] = query_ref[:, h * HEAD_DIM : (h + 1) * HEAD_DIM]
     for k in range(1, cols):
@@ -168,6 +175,13 @@
 
     lax.fori_loop(0, pairs, near_pass, 0)
 
+    listed = lists_ref[col, pl.ds(group, 1), :]
+
+    def bias_of(source):
+        inside = (listed >= source * local_blocks) & (listed < (source + 1) * local_blocks)
+        found = jnp.max(jnp.where(inside, 1.0, 0.0), axis=1, keepdims=True)
+        return jnp.broadcast_to(jnp.where(found > 0.5, 0.0, -1e30), (1, BLK))
+
     batch = 4
     for first in range(0, devices, batch):
         bias = []
@@ -175,8 +189,10 @@
             k = order[slot]
             if k:
                 block_copy(k).wait()
+            else:
+                own_block.wait()
             peer_row, peer_col = peer(k)
-            bias.append(bias_ref[peer_row * cols + peer_col])
+            bias.append(bias_of(peer_row * cols + peer_col))
         bias = jnp.concatenate(bias, axis=1)
 
         def far_pass(p, carry):
@@ -211,42 +227,15 @@
             out_ref[p, :, h * HEAD_DIM : (h + 1) * HEAD_DIM] = result[p * halves : (p + 1) * halves]
 
 
-def attend(queries, blocks, bias, stretch_keys, stretch_values, tokens):
-    rows = lax.axis_size("row")
-    cols = lax.axis_size("col")
-    devices = rows * cols
-    lines = BLK * queries.shape[1] // HEAD_DIM
-    vmem = pl.BlockSpec(memory_space=pltpu.VMEM)
-    hbm = pl.BlockSpec(memory_space=pl.ANY)
-    dma = pltpu.SemaphoreType.DMA
-    return pl.pallas_call(
-        functools.partial(attend_kernel, rows, cols),
-        out_shape=jax.ShapeDtypeStruct((BLK // tokens, tokens, queries.shape[1]), jnp.bfloat16),
-        in_specs=[vmem, vmem, vmem, hbm, hbm],
-        out_specs=vmem,
-        scratch_shapes=[
-            pltpu.VMEM((devices, 2, BLK, HEAD_DIM), jnp.bfloat16),
-            pltpu.VMEM((cols, 2, BLK, HEAD_DIM), jnp.bfloat16),
-            pltpu.VMEM((lines, HEAD_DIM), jnp.bfloat16),
-            pltpu.VMEM((lines, HEAD_DIM), jnp.float32),
-            pltpu.VMEM((lines, HEAD_DIM), jnp.float32),
-            pltpu.VMEM((lines, HEAD_DIM), jnp.float32),
-            dma((2,)),
-            dma((cols - 1,)),
-            dma((cols - 1,)),
-            dma((devices,)),
-            dma((devices,)),
-        ],
-        compiler_params=pltpu.CompilerParams(
-            collective_id=1, has_side_effects=True, vmem_limit_bytes=40 * 1024 * 1024
-        ),
-    )(queries, blocks, bias, stretch_keys, stretch_values)
-
-
-def tail_kernel(
+def layer_kernel(
     cols,
     rows,
-    att_ref,
+    local_blocks,
+    query_ref,
+    block_ref,
+    lists_ref,
+    near_key_ref,
+    near_value_ref,
     wo_ref,
     res_ref,
     gain_ref,
@@ -257,6 +246,13 @@
     gate_buf,
     up_buf,
     down_buf,
+    held,
+    near,
+    heads_first,
+    top,
+    norm,
+    acc,
+    att_ref,
     att_buf,
     part,
     first,
@@ -281,6 +277,11 @@
     up_sem,
     down_sem,
     wo_sem,
+    near_sem,
+    near_send,
+    near_recv,
+    block_send,
+    block_recv,
     att_send,
     att_recv,
     rs_pair_send,
@@ -365,8 +366,8 @@
 
     def rs_pair(w, q):
         return remote(
-            part.at[w, q, :, 1 - core],
-            first.at[w, q],
+            part.at[q, :, 1 - core],
+            first.at[q],
             rs_pair_send.at[w, q],
             rs_pair_recv.at[w, q],
             "row",
@@ -375,8 +376,8 @@
 
     def rs_line(w, q, k):
         return remote(
-            mid.at[w, q, layer(k)],
-            second.at[w, q, k - 1],
+            mid.at[q, layer(k)],
+            second.at[q, k - 1],
             rs_line_send.at[w, q, k - 1],
             rs_line_recv.at[w, q, k - 1],
             "row",
@@ -386,8 +387,8 @@
     def rs_middle(w, q):
         rs_pair(w, q).wait()
         for d in range(row_lines):
-            mid[w, q, d] = (
-                part[w, q, d, core].astype(jnp.float32) + first[w, q, d].astype(jnp.float32)
+            mid[q, d] = (
+                part[q, d, core].astype(jnp.float32) + first[q, d].astype(jnp.float32)
             ).astype(jnp.bfloat16)
 
     def rs_lines_start(w, q):
@@ -395,10 +396,10 @@
             rs_line(w, q, k).start()
 
     def rs_finish(w, q):
-        result = mid[w, q, depth_me].astype(jnp.float32)
+        result = mid[q, depth_me].astype(jnp.float32)
         for k in range(1, row_lines):
             rs_line(w, q, k).wait()
-            result = result + second[w, q, k - 1].astype(jnp.float32)
+            result = result + second[q, k - 1].astype(jnp.float32)
         return result
 
     def square_copy(q, k):
@@ -446,7 +447,7 @@
             square_copy(q, k).wait()
             squares = squares + square_buf[q, k - 1]
         factor = lax.rsqrt(squares / (width * cols) + 1e-05)[:, :1]
-        pieces[q, depth_me, core] = (stream[q] * factor * gain_ref[...].astype(jnp.float32)).astype(
+        pieces[q, depth_me, core] = (stream[q] * factor * gain_ref[...].astype(jnp.float32)[None, :]).astype(
             jnp.bfloat16
         )
         for k in range(1, row_lines):
@@ -462,13 +463,15 @@
         for k in range(row_lines):
             ag_pair(q, k).wait()
 
-    def transfers(stage, slot):
+    def transfers(stage, step):
+        slot = lax.rem(step, SLOTS)
+        hold = lax.rem(step, HOLD)
         if stage == 0:
-            pair = (gate_part.at[slot, 1 - pair_me], gate_first.at[slot])
-            along = [(up_part.at[slot, line(k)], up_first.at[slot, k - 1]) for k in range(1, col_lines)]
+            pair = (gate_part.at[hold, 1 - pair_me], gate_first.at[slot])
+            along = [(up_part.at[hold, line(k)], up_first.at[slot, k - 1]) for k in range(1, col_lines)]
         elif stage == 1:
-            pair = (up_mid.at[slot, 1 - pair_me], up_second.at[slot])
-            along = [(gate_mid.at[slot, line(k)], gate_second.at[slot, k - 1]) for k in range(1, col_lines)]
+            pair = (up_mid.at[hold, 1 - pair_me], up_second.at[slot])
+            along = [(gate_mid.at[hold, line(k)], gate_second.at[slot, k - 1]) for k in range(1, col_lines)]
         elif stage == 2:
             pair = (left.at[slot, 0, 0], left.at[slot, 0, 1])
             along = [(right.at[slot, 0, 0], right.at[slot, 0, k]) for k in range(1, col_lines)]
@@ -492,22 +495,37 @@
 
     for p in range(spare):
         wo_copy(p).start()
-    for j in range(steps):
-        gate_copy(j).start()
-        up_copy(j).start()
-        if j < steps - spare:
+
+    def begin():
+        for j in range(steps):
+            gate_copy(j).start()
+            up_copy(j).start()
+        for j in range(steps - spare):
             down_copy(j).start()
-    barrier = pltpu.get_barrier_semaphore()
-    for k in range(1, cols):
-        pl.semaphore_signal(
-            barrier, inc=1, device_id={"col": lax.rem(col + k, cols)}, device_id_type=MESH
-        )
-    pl.semaphore_signal(barrier, inc=1, device_id={"row": row_other}, device_id_type=MESH)
-    for k in range(1, row_lines):
-        pl.semaphore_signal(
-            barrier, inc=1, device_id={"row": layer(k) * 2 + core}, device_id_type=MESH
-        )
-    pl.semaphore_wait(barrier, cols - 1 + row_lines)
+
+    attention(
+        rows,
+        cols,
+        local_blocks,
+        begin,
+        query_ref,
+        block_ref,
+        lists_ref,
+        near_key_ref,
+        near_value_ref,
+        att_ref,
+        held,
+        near,
+        heads_first,
+        top,
+        norm,
+        acc,
+        near_sem,
+        near_send,
+        near_recv,
+        block_send,
+        block_recv,
+    )
     for q in range(NC):
         for k in range(1, cols):
             att_copy(q, k).start()
@@ -515,7 +533,7 @@
     for p in range(spare):
         wo_copy(p).wait()
 
-    for q in range(NC):
+    def project(q):
         att_buf[q, col] = att_ref[:, q * toks : (q + 1) * toks, :]
         for k in range(1, cols):
             att_copy(q, k).wait()
@@ -528,25 +546,34 @@
                     down_buf[steps - spare + p, :, start : start + tile],
                     preferred_element_type=jnp.float32,
                 )
-            part[0, q, :, :, :, start : start + tile] = product.astype(jnp.bfloat16).reshape(
+            part[q, :, :, :, start : start + tile] = product.astype(jnp.bfloat16).reshape(
                 row_lines, 2, toks, tile
             )
         rs_pair(0, q).start()
-        rs_middle(0, q)
-        if q == 0:
-            rs_lines_start(0, 0)
+
+    project(0)
+    rs_middle(0, 0)
+    rs_lines_start(0, 0)
+    project(1)
+    rs_middle(0, 1)
+    rs_lines_start(0, 1)
+    stream_step(0)
+    norm_step(0)
+    stream_step(1)
+    norm_step(1)
+    for q in range(2, NC):
+        project(q)
     for j in range(steps - spare, steps):
         down_copy(j).start()
-    stream_step(0)
-    norm_step(0)
-    if NC > 1:
-        rs_lines_start(0, 1)
+    for q in range(2, NC):
+        rs_middle(0, q)
     ag_forward(0)
+    rs_lines_start(0, 2)
 
     chunks = NC * steps
 
     def stage_when(i, stage):
-        return pl.when((i >= stage) & (i < chunks + stage))
+        return pl.when((i >= LAGS[stage]) & (i < chunks + LAGS[stage]))
 
     def iteration(i, carry):
         q_now = i // steps
@@ -563,65 +590,69 @@
                 gate_copy(i).wait()
                 up_copy(i).wait()
 
-            slot = lax.rem(i, SLOTS)
+            hold = lax.rem(i, HOLD)
             inputs = pieces[q_now].reshape(many, pieces.shape[-1])
             product = jnp.dot(inputs, gate_buf[j_now], preferred_element_type=jnp.float32).astype(jnp.bfloat16)
             for b in range(cols):
-                gate_part[slot, b % 2, b // 2] = product[b * share : (b + 1) * share]
+                gate_part[hold, b % 2, b // 2] = product[b * share : (b + 1) * share]
             product = jnp.dot(inputs, up_buf[j_now], preferred_element_type=jnp.float32).astype(jnp.bfloat16)
             for b in range(cols):
-                up_part[slot, b // 2, b % 2] = product[b * share : (b + 1) * share]
-            for copy in transfers(0, slot):
+                up_part[hold, b // 2, b % 2] = product[b * share : (b + 1) * share]
+            for copy in transfers(0, i):
                 copy.start()
 
         @stage_when(i, 1)
         def _():
-            slot = lax.rem(i - 1, SLOTS)
-            for copy in transfers(0, slot):
+            step = i - LAGS[1]
+            slot = lax.rem(step, SLOTS)
+            hold = lax.rem(step, HOLD)
+            for copy in transfers(0, step):
                 copy.wait()
-            gate_mid[slot] = (
-                gate_part[slot, pair_me].astype(jnp.float32) + gate_first[slot].astype(jnp.float32)
+            gate_mid[hold] = (
+                gate_part[hold, pair_me].astype(jnp.float32) + gate_first[slot].astype(jnp.float32)
             ).astype(jnp.bfloat16)
-            up_sum = up_part[slot, line_me].astype(jnp.float32)
+            up_sum = up_part[hold, line_me].astype(jnp.float32)
             for k in range(1, col_lines):
                 up_sum = up_sum + up_first[slot, k - 1].astype(jnp.float32)
-            up_mid[slot] = up_sum.astype(jnp.bfloat16)
-            for copy in transfers(1, slot):
+            up_mid[hold] = up_sum.astype(jnp.bfloat16)
+            for copy in transfers(1, step):
                 copy.start()
 
         @stage_when(i, 2)
         def _():
-            slot = lax.rem(i - 2, SLOTS)
-            for copy in transfers(1, slot):
+            step = i - LAGS[2]
+            slot = lax.rem(step, SLOTS)
+            hold = lax.rem(step, HOLD)
+            for copy in transfers(1, step):
                 copy.wait()
-            gate = gate_mid[slot, line_me].astype(jnp.float32)
+            gate = gate_mid[hold, line_me].astype(jnp.float32)
             for k in range(1, col_lines):
                 gate = gate + gate_second[slot, k - 1].astype(jnp.float32)
-            up = up_mid[slot, pair_me].astype(jnp.float32) + up_second[slot].astype(jnp.float32)
+            up = up_mid[hold, pair_me].astype(jnp.float32) + up_second[slot].astype(jnp.float32)
             hidden = (gate / (1.0 + jnp.exp(-gate)) * up).astype(jnp.bfloat16)
             left[slot, 0, 0] = hidden[:, :half]
             right[slot, 0, 0] = hidden[:, half:]
-            for copy in transfers(2, slot):
+            for copy in transfers(2, step):
                 copy.start()
 
         @stage_when(i, 3)
         def _():
-            slot = lax.rem(i - 3, SLOTS)
-            for copy in transfers(2, slot):
+            for copy in transfers(2, i - LAGS[3]):
                 copy.wait()
-            for copy in transfers(3, slot):
+            for copy in transfers(3, i - LAGS[3]):
                 copy.start()
 
         @stage_when(i, 4)
         def _():
-            j = lax.rem(i - 4, steps)
-            slot = lax.rem(i - 4, SLOTS)
-
-            @pl.when(i - 4 < steps)
+            step = i - LAGS[4]
+            j = lax.rem(step, steps)
+            slot = lax.rem(step, SLOTS)
+
+            @pl.when(step < steps)
             def _():
-                down_copy(i - 4).wait()
-
-            for copy in transfers(3, slot):
+                down_copy(step).wait()
+
+            for copy in transfers(3, step):
                 copy.wait()
             gathered = jnp.concatenate(
                 [
@@ -638,55 +669,68 @@
                     preferred_element_type=jnp.float32,
                 )
 
-        @pl.when((j_now == 1) & (q_now + 1 < NC))
-        def _():
-            stream_step(q_now + 1)
-
-        @pl.when((j_now == 2) & (q_now + 1 < NC))
-        def _():
-            norm_step(q_now + 1)
+        @pl.when((j_now == 1) & (q_now + 2 < NC))
+        def _():
+            stream_step(q_now + 2)
 
         @pl.when((j_now == 2) & (q_now + 2 < NC))
         def _():
-            rs_lines_start(0, q_now + 2)
-
-        @pl.when((j_now == 5) & (q_now + 1 < NC))
+            norm_step(q_now + 2)
+
+        @pl.when((j_now == 2) & (q_now + 3 < NC))
+        def _():
+            rs_lines_start(0, q_now + 3)
+
+        @pl.when((j_now == 4) & (q_now + 1 < NC))
         def _():
             ag_forward(q_now + 1)
 
-        @pl.when((i >= steps + 3) & (lax.rem(i - 3, steps) == 0))
-        def _():
-            q = (i - 4) // steps
+        done = i - LAGS[4] + 1
+        q_done = done // steps - 1
+
+        @pl.when((done > 0) & (lax.rem(done, steps) == 0))
+        def _():
             for p in range(2):
                 for k in range(col_lines):
                     owner = line(col_lines - k) * 2 + lax.rem(pair_me + p, 2)
                     begin = (p * col_lines + k) * share
-                    part[1, q, owner] = (
+                    part[q_done, owner] = (
                         total[begin : begin + share, :].astype(jnp.bfloat16).reshape(2, toks, width)
                     )
-            rs_pair(1, q).start()
+            rs_pair(1, q_done).start()
             total[...] = jnp.zeros_like(total)
 
-        @pl.when((i >= steps + 4) & (lax.rem(i - 4, steps) == 0))
-        def _():
-            q = (i - 5) // steps
-            rs_middle(1, q)
-            rs_lines_start(1, q)
-
-        @pl.when((i >= steps + 8) & (lax.rem(i - 8, steps) == 0))
-        def _():
-            q = (i - 9) // steps
-            out_ref[q] = stream[q] + rs_finish(1, q)
+        @pl.when((done > steps) & (lax.rem(done, steps) == 1))
+        def _():
+            rs_middle(1, q_done)
+            rs_lines_start(1, q_done)
+
+        @pl.when((done > steps) & (lax.rem(done, steps) == 5))
+        def _():
+            out_ref[q_done] = stream[q_done] + rs_finish(1, q_done)
 
         return carry
 
-    lax.fori_loop(0, chunks + 4, iteration, 0)
+    lax.fori_loop(0, chunks + LAGS[4], iteration, 0)
     rs_middle(1, NC - 1)
     rs_lines_start(1, NC - 1)
     out_ref[NC - 1] = stream[NC - 1] + rs_finish(1, NC - 1)
 
 
-def tail(attended, out_weight, residual, norm_gain, gate_weight, up_weight, down_weight):
+def layer_call(
+    queries,
+    blocks,
+    block_lists,
+    local_blocks,
+    stretch_keys,
+    stretch_values,
+    out_weight,
+    residual,
+    norm_gain,
+    gate_weight,
+    up_weight,
+    down_weight,
+):
     cols = lax.axis_size("col")
     rows = lax.axis_size("row")
     depth, hidden_width = gate_weight.shape
@@ -697,6 +741,8 @@
     share = rows * toks // cols
     col_lines = cols // 2
     row_lines = rows // 2
+    devices = rows * cols
+    lines = BLK * inner // HEAD_DIM
     assert rows == 2 * cols and inner % wide == 0
     vmem = pl.BlockSpec(memory_space=pltpu.VMEM)
     hbm = pl.BlockSpec(memory_space=pl.ANY)
@@ -706,29 +752,36 @@
         return pltpu.VMEM(shape, jnp.bfloat16)
 
     out = pl.pallas_call(
-        functools.partial(tail_kernel, cols, rows),
+        functools.partial(layer_kernel, cols, rows, local_blocks),
         out_shape=jax.ShapeDtypeStruct((NC, toks, width), jnp.float32),
-        in_specs=[vmem, hbm, vmem, vmem, hbm, hbm, hbm],
+        in_specs=[vmem, hbm, vmem, hbm, hbm, hbm, vmem, vmem, hbm, hbm, hbm],
         out_specs=vmem,
         scratch_shapes=[
             held(STEPS, depth, wide),
             held(STEPS, depth, wide),
             held(STEPS, wide, width),
+            held(devices, 2, BLK, HEAD_DIM),
+            held(cols, 2, BLK, HEAD_DIM),
+            held(lines, HEAD_DIM),
+            pltpu.VMEM((lines, HEAD_DIM), jnp.float32),
+            pltpu.VMEM((lines, HEAD_DIM), jnp.float32),
+            pltpu.VMEM((lines, HEAD_DIM), jnp.float32),
+            held(BLK // tokens, tokens, inner),
             held(NC, cols, 2, toks, inner),
-            held(2, NC, row_lines, 2, toks, width),
-            held(2, NC, row_lines, toks, width),
-            held(2, NC, row_lines, toks, width),
-            held(2, NC, row_lines - 1, toks, width),
+            held(NC, row_lines, 2, toks, width),
+            held(NC, row_lines, toks, width),
+            held(NC, row_lines, toks, width),
+            held(NC, row_lines - 1, toks, width),
             pltpu.VMEM((NC, toks, width), jnp.float32),
             pltpu.VMEM((NC, toks, 128), jnp.float32),
             pltpu.VMEM((NC, cols - 1, toks, 128), jnp.float32),
             held(NC, row_lines, 2, toks, depth),
-            held(SLOTS, 2, col_lines, share, wide),
-            held(SLOTS, col_lines, 2, share, wide),
+            held(HOLD, 2, col_lines, share, wide),
+            held(HOLD, col_lines, 2, share, wide),
             held(SLOTS, col_lines, share, wide),
             held(SLOTS, col_lines - 1, 2, share, wide),
-            held(SLOTS, col_lines, share, wide),
-            held(SLOTS, 2, share, wide),
+            held(HOLD, col_lines, share, wide),
+            held(HOLD, 2, share, wide),
             held(SLOTS, col_lines - 1, share, wide),
             held(SLOTS, share, wide),
             held(SLOTS, col_lines, 2, share, wide // 2),
@@ -738,6 +791,11 @@
             dma((STEPS,)),
             dma((STEPS,)),
             dma((inner // wide,)),
+            dma((3,)),
+            dma((cols - 1,)),
+            dma((cols - 1,)),
+            dma((devices,)),
+            dma((devices,)),
             dma((NC, cols - 1)),
             dma((NC, cols - 1)),
             dma((2, NC)),
@@ -759,10 +817,14 @@
             collective_id=0, has_side_effects=True, vmem_limit_bytes=66 * 1000 * 1000
         ),
     )(
-        attended,
+        queries,
+        blocks,
+        block_lists,
+        stretch_keys,
+        stretch_values,
         out_weight,
         residual.reshape(NC, toks, width),
-        norm_gain.reshape(1, width),
+        norm_gain,
         gate_weight,
         up_weight,
         down_weight,
@@ -791,18 +853,23 @@
     device_count = row_count * col_count
     my_index = row_index * col_count + col_index
     local_blocks = cache_keys.shape[1] // BLK
-    heads_here = queries.shape[1] // HEAD_DIM
-    lists = jnp.swapaxes(block_lists, 0, 1)
-    lists = jnp.repeat(lists, row_count // KV_HEADS, axis=0).reshape(device_count, -1)
-    matched = lists // local_blocks == my_index
-    block_rows = jnp.sum(jnp.where(matched, lists % local_blocks, 0), axis=1)
-    blocks = gather_blocks(block_rows, cache_keys, cache_values)
-    my_list = block_lists[col_index, row_index * heads_here // GROUP]
-    sources = jnp.arange(device_count, dtype=jnp.int32)
-    wanted = jnp.any(my_list[None, :] // local_blocks == sources[:, None], axis=1)
-    bias = jnp.broadcast_to(jnp.where(wanted, 0.0, -1e30)[:, None, None], (device_count, 1, BLK))
-    attended = attend(queries, blocks, bias, stretch_keys, stretch_values, residual.shape[0])
-    return tail(attended, out_weight, residual, norm_gain, gate_weight, up_weight, down_weight)
+    matched = block_lists // local_blocks == my_index
+    block_rows = jnp.sum(jnp.where(matched, block_lists % local_blocks, 0), axis=2)
+    blocks = gather_blocks(block_rows, cache_keys, cache_values, device_count)
+    return layer_call(
+        queries,
+        blocks,
+        block_lists,
+        local_blocks,
+        stretch_keys,
+        stretch_values,
+        out_weight,
+        residual,
+        norm_gain,
+        gate_weight,
+        up_weight,
+        down_weight,
+    )
 
 
 def solution(mesh):

time: 222 us -> 203 us (0.914)
  Pallas kernels: 214 us -> 200 us
  local copies, waits for them, and re-layouts: 4.76 us -> 0 us
    pallas_call x3 -> x2, Pallas kernels: 214 us -> 200 us  [the longest x1 195 us: layer_call(): pl.pallas_call(functools.partial(layer_kernel, cols, rows, local_blocks),...]
    unnamed x14 -> x0, local copies, waits for them, and re-layouts: 3.9 us -> none
where the time goes in v3:
time: 203 us
  Pallas kernels  200 us (99%)
  other arithmetic  3.22 us (2%)
    pallas_call x1, Pallas kernels, layer_call(): pl.pallas_call(functools.partial(layer_kernel, cols, rows, local_blocks),...  195 us
    pallas_call x1, Pallas kernels, gather_blocks(): pl.pallas_call(gather_kernel, out_shape=jax.ShapeDtypeStruct((devices, 2,...  4.4 us

profile of v3, /device:TPU:0, one launch (start us, length us, event | category | flops | bytes accessed | tf_op | source)
XLA Modules:
  0.0 203.0 jit_solution(13598388406309879344)
XLA Ops:
  0.0 1.5 fusion.2.rows_ref
  1.5 4.4 %shard_map.118.block_ref = bf16[32,2,128,128]{3,2,1,0:T(8,128)(2,1)} custom-call(s32[4,8]{1,0:T(4,128)} %fusion.2.rows_ref, bf16[8,1024,128]{2,1,0:T(8,128)(2,1)} %keys_ref.1, bf16[8,1024,128]{2,1,0:T(8,128)(2,1)} %values_ref.1), custom_call_target="tpu_custom_call" | custom-call | tf_op jit(solution)/shard_map/pallas_call | solution.py:46
  5.9 195.3 %shard_map.119 = f32[4,16,2048]{2,1,0:T(8,128)} custom-call(bf16[128,1024]{1,0:T(8,128)(2,1)} %query_ref.1, bf16[32,2,128,128]{3,2,1,0:T(8,128)(2,1)} %shard_map.118.block_ref, s32[4,8,16]{2,1,0:T(8,128)} %lists_ref.1, bf16[8,128,128]{2,1,0:T(8,128)(2,1)} %near_key_ref.1, bf16[8,128,128]{2,1,0:T(8,128)(2,1)} %near_value_ref.1, bf16[1024,2048]{1,0:T(8,128)(2,1)} %wo_ref.1, ...), custom_call_target="tpu_custom_call" | custom-call | tf_op jit(solution)/shard_map/pallas_call | solution.py:754
  201.2 1.8 convert_element_type.6

commit v4 on v3

--- a/solution.py
+++ b/solution.py
@@ -80,40 +80,75 @@
     out_ref,
     held,
     near,
-    heads_first,
+    turned,
     top,
     norm,
     acc,
+    stats,
     near_sem,
     near_send,
     near_recv,
     block_send,
     block_recv,
+    swap_send,
+    swap_recv,
 ):
     row = lax.axis_index("row")
     col = lax.axis_index("col")
     devices = rows * cols
+    layers = rows // 2
+    plane = 2 * cols
+    depth = row // 2
+    core = lax.rem(row, 2)
+    low = layers // 2 - 1
+    high = layers // 2
     heads = query_ref.shape[1] // HEAD_DIM
-    group = row * heads // GROUP
     scaling = 1.0 / math.sqrt(HEAD_DIM)
-    pairs = heads // 2
-    order = sorted(range(devices), key=lambda k: (k // cols // 2, k))
-    slot_of = {k: s for s, k in enumerate(order)}
-
-    def peer(k):
-        return flipped(row, k // cols), flipped(col, k % cols)
-
-    def block_copy(k):
-        peer_row, peer_col = peer(k)
-        slot = slot_of[k]
+    lines = heads * BLK
+    strip = min(256, lines)
+
+    def is_middle(d):
+        return jnp.where((d == low) | (d == high), 1, 0)
+
+    paired = is_middle(depth)
+    my_middle = low + depth // high
+    mirror_row = (layers - 1 - depth) * 2 + core
+
+    def differing(index, bits, size):
+        result = 0
+        place = 1
+        while place < size:
+            one = lax.rem(index // place, 2)
+            two = lax.rem(bits // place, 2)
+            result = result + place * (one + two - 2 * one * two)
+            place *= 2
+        return result
+
+    def block_parts(kz, e):
+        target_depth = flipped(depth, kz)
+        target_core = flipped(core, e // cols)
+        target_col = flipped(col, e % cols)
+        host = target_depth + is_middle(target_depth) * (my_middle - target_depth)
+        block = (target_depth * 2 + target_core) * cols + target_col
+        return block, host * 2 + target_core, target_col, kz * plane + e
+
+    def block_copy(kz, e):
+        block, host_row, host_col, slot = block_parts(kz, e)
         return pltpu.make_async_remote_copy(
-            src_ref=block_ref.at[peer_row * cols + peer_col],
+            src_ref=block_ref.at[block],
             dst_ref=held.at[slot],
             send_sem=block_send.at[slot],
             recv_sem=block_recv.at[slot],
-            device_id={"row": peer_row, "col": peer_col},
+            device_id={"row": host_row, "col": host_col},
             device_id_type=MESH,
         )
+
+    def own_block(kz):
+        block, _, _, slot = block_parts(kz, 0)
+        return pltpu.make_async_copy(block_ref.at[block], held.at[slot], block_recv.at[slot])
+
+    def arrived(slot):
+        return pltpu.make_async_copy(block_ref.at[0], held.at[slot], block_recv.at[slot])
 
     def near_copy(k):
         return pltpu.make_async_remote_copy(
@@ -125,106 +160,184 @@
             device_id_type=MESH,
         )
 
+    def swap(src, dst, index):
+        return pltpu.make_async_remote_copy(
+            src_ref=src,
+            dst_ref=dst,
+            send_sem=swap_send.at[index],
+            recv_sem=swap_recv.at[index],
+            device_id={"row": mirror_row},
+            device_id_type=MESH,
+        )
+
+    query_swap = swap(turned.at[0], turned.at[1], 0)
+    result_swap = swap(turned.at[1], turned.at[2], 1)
+    stats_swap = swap(stats.at[0], stats.at[1], 2)
+
+    group = row * heads // GROUP
     own = (
         pltpu.make_async_copy(near_key_ref.at[group], near.at[col, 0], near_sem.at[0]),
         pltpu.make_async_copy(near_value_ref.at[group], near.at[col, 1], near_sem.at[1]),
     )
-    own_block = pltpu.make_async_copy(block_ref.at[row * cols + col], held.at[0], near_sem.at[2])
     for copy in own:
         copy.start()
-    own_block.start()
+    for h in range(heads):
+        block = query_ref[:, h * HEAD_DIM : (h + 1) * HEAD_DIM].astype(jnp.float32)
+        turned[0, :, h * BLK : (h + 1) * BLK] = jnp.transpose(block).astype(jnp.bfloat16)
     barrier = pltpu.get_barrier_semaphore()
     for k in range(1, devices):
-        peer_row, peer_col = peer(k)
         pl.semaphore_signal(
-            barrier, inc=1, device_id={"row": peer_row, "col": peer_col}, device_id_type=MESH
+            barrier,
+            inc=1,
+            device_id={"row": flipped(row, k // cols), "col": flipped(col, k % cols)},
+            device_id_type=MESH,
         )
     pl.semaphore_wait(barrier, devices - 1)
+
+    @pl.when(paired == 1)
+    def _():
+        query_swap.start()
+
+    for kz in list(range(high, layers)) + list(range(high)):
+        for e in range(plane):
+            if e:
+                block_copy(kz, e).start()
+            elif kz == 0:
+                own_block(0).start()
+            elif kz == layers - 1:
+
+                @pl.when(paired == 1)
+                def _():
+                    own_block(layers - 1).start()
+
+                @pl.when(paired == 0)
+                def _():
+                    block_copy(layers - 1, 0).start()
+            else:
+                block_copy(kz, e).start()
     for copy in own:
         copy.wait()
     for k in range(1, cols):
         near_copy(k).start()
-    for k in order[1:]:
-        block_copy(k).start()
     begin()
-    for h in range(heads):
-        heads_first[h * BLK : (h + 1) * BLK, :] = query_ref[:, h * HEAD_DIM : (h + 1) * HEAD_DIM]
+    top[1] = jnp.full(top.shape[1:], -1e30, jnp.float32)
+    norm[1] = jnp.zeros(norm.shape[1:], jnp.float32)
+    acc[1] = jnp.zeros(acc.shape[1:], jnp.float32)
     for k in range(1, cols):
         near_copy(k).wait()
 
-    def near_pass(p, carry):
-        lines = pl.ds(pl.multiple_of(p * 2 * BLK, 2 * BLK), 2 * BLK)
-        keys = near[:, 0].reshape(cols * BLK, HEAD_DIM)
-        scores = lax.dot_general(
-            heads_first[lines, :], keys, (((1,), (1,)), ((), ())), preferred_element_type=jnp.float32
-        ) * scaling
-        position = lax.broadcasted_iota(jnp.int32, scores.shape, 1)
-        token = col * BLK + lax.rem(lax.broadcasted_iota(jnp.int32, scores.shape, 0), BLK)
+    def weighted(values, weights):
+        return lax.dot_general(
+            values,
+            weights.astype(jnp.bfloat16),
+            (((0,), (0,)), ((), ())),
+            preferred_element_type=jnp.float32,
+        )
+
+    near_keys = near[:, 0].reshape(cols * BLK, HEAD_DIM)
+    near_values = near[:, 1].reshape(cols * BLK, HEAD_DIM)
+    for begin_at in range(0, lines, strip):
+        part = slice(begin_at, begin_at + strip)
+        scores = jnp.dot(near_keys, turned[0, :, part], preferred_element_type=jnp.float32) * scaling
+        position = lax.broadcasted_iota(jnp.int32, scores.shape, 0)
+        token = col * BLK + lax.rem(lax.broadcasted_iota(jnp.int32, scores.shape, 1), BLK)
         allowed = position <= token
         scores = jnp.where(allowed, scores, -1e30)
-        new_top = jnp.max(scores, axis=1, keepdims=True)
+        new_top = jnp.max(scores, axis=0, keepdims=True)
         weights = jnp.where(allowed, jnp.exp(scores - new_top), 0.0)
-        top[lines, :] = jnp.broadcast_to(new_top, (2 * BLK, HEAD_DIM))
-        norm[lines, :] = jnp.broadcast_to(jnp.sum(weights, axis=1, keepdims=True), (2 * BLK, HEAD_DIM))
-        acc[lines, :] = jnp.dot(
-            weights.astype(jnp.bfloat16),
-            near[:, 1].reshape(cols * BLK, HEAD_DIM),
-            preferred_element_type=jnp.float32,
-        )
+        top[0, :, part] = new_top
+        norm[0, :, part] = jnp.sum(weights, axis=0, keepdims=True)
+        acc[0, :, part] = weighted(near_values, weights)
+
+    batch = 4
+    turns = plane // batch
+
+    @pl.when(paired == 1)
+    def _():
+        query_swap.wait()
+
+    def far_batch(index, carry):
+        turn = index // turns
+        kz = lax.rem(turn + high, layers)
+        first = kz * plane + lax.rem(index, turns) * batch
+        shared = paired * (kz // high)
+        problem_row = row + shared * (mirror_row - row)
+        listed = lists_ref[col, pl.ds(problem_row * heads // GROUP, 1), :]
+        source_depth = differing(depth, kz + shared * (layers - 1 - 2 * kz), layers)
+        bias = []
+        for j in range(batch):
+            e = lax.rem(first + j, plane)
+            source = (source_depth * 2 + differing(core, e // cols, 2)) * cols + differing(
+                col, lax.rem(e, cols), cols
+            )
+            inside = (listed >= source * local_blocks) & (listed < (source + 1) * local_blocks)
+            found = jnp.max(jnp.where(inside, 1.0, 0.0), axis=1, keepdims=True)
+            bias.append(jnp.broadcast_to(jnp.where(found > 0.5, 0.0, -1e30), (BLK, strip)))
+        bias = jnp.concatenate(bias, axis=0)
+        for j in range(batch):
+            arrived(first + j).wait()
+
+        keys = held[pl.ds(first, batch), 0].reshape(batch * BLK, HEAD_DIM)
+        values = held[pl.ds(first, batch), 1].reshape(batch * BLK, HEAD_DIM)
+        parts = [slice(begin_at, begin_at + strip) for begin_at in range(0, lines, strip)]
+        tops, norms, accs = [], [], []
+        for part in parts:
+            scores = jnp.dot(keys, turned[shared, :, part], preferred_element_type=jnp.float32) * scaling + bias
+            old_top = top[shared, :, part]
+            new_top = jnp.maximum(old_top, jnp.max(scores, axis=0, keepdims=True))
+            decay = jnp.exp(old_top - new_top)
+            weights = jnp.exp(scores - new_top)
+            tops.append(new_top)
+            norms.append(norm[shared, :, part] * decay + jnp.sum(weights, axis=0, keepdims=True))
+            accs.append(acc[shared, :, part] * decay + weighted(values, weights))
+        for n, part in enumerate(parts):
+            top[shared, :, part] = tops[n]
+            norm[shared, :, part] = norms[n]
+            acc[shared, :, part] = accs[n]
         return carry
 
-    lax.fori_loop(0, pairs, near_pass, 0)
-
-    listed = lists_ref[col, pl.ds(group, 1), :]
-
-    def bias_of(source):
-        inside = (listed >= source * local_blocks) & (listed < (source + 1) * local_blocks)
-        found = jnp.max(jnp.where(inside, 1.0, 0.0), axis=1, keepdims=True)
-        return jnp.broadcast_to(jnp.where(found > 0.5, 0.0, -1e30), (1, BLK))
-
-    batch = 4
-    for first in range(0, devices, batch):
-        bias = []
-        for slot in range(first, first + batch):
-            k = order[slot]
-            if k:
-                block_copy(k).wait()
-            else:
-                own_block.wait()
-            peer_row, peer_col = peer(k)
-            bias.append(bias_of(peer_row * cols + peer_col))
-        bias = jnp.concatenate(bias, axis=1)
-
-        def far_pass(p, carry):
-            lines = pl.ds(pl.multiple_of(p * 2 * BLK, 2 * BLK), 2 * BLK)
-            keys = held[first : first + batch, 0].reshape(batch * BLK, HEAD_DIM)
-            scores = (
-                lax.dot_general(
-                    heads_first[lines, :], keys, (((1,), (1,)), ((), ())), preferred_element_type=jnp.float32
-                )
-                * scaling
-                + bias
-            )
-            old_top = top[lines, :]
-            new_top = jnp.maximum(old_top, jnp.max(scores, axis=1, keepdims=True))
-            decay = jnp.exp(old_top - new_top)
-            weights = jnp.exp(scores - new_top[:, :1])
-            top[lines, :] = new_top
-            norm[lines, :] = norm[lines, :] * decay + jnp.sum(weights, axis=1, keepdims=True)
-            acc[lines, :] = acc[lines, :] * decay + jnp.dot(
-                weights.astype(jnp.bfloat16),
-                held[first : first + batch, 1].reshape(batch * BLK, HEAD_DIM),
-                preferred_element_type=jnp.float32,
-            )
-            return carry
-
-        lax.fori_loop(0, pairs, far_pass, 0)
+    lax.fori_loop(0, (layers - high) * turns, far_batch, 0)
+
+    @pl.when(paired == 1)
+    def _():
+        turned[1] = (acc[1] / norm[1]).astype(jnp.bfloat16)
+        stats[0, 0:1, :] = top[1]
+        stats[0, 1:2, :] = norm[1]
+        stats_swap.start()
+        result_swap.start()
+
+    lax.fori_loop((layers - high) * turns, layers * turns, far_batch, 0)
+
+    @pl.when(paired == 1)
+    def _():
+        stats_swap.wait()
+        result_swap.wait()
+        other_top = stats[1, 0:1, :]
+        own_top = top[0]
+        both = jnp.maximum(own_top, other_top)
+        own_part = jnp.exp(own_top - both)
+        other_part = jnp.exp(other_top - both) * stats[1, 1:2, :]
+        norm[0] = norm[0] * own_part + other_part
+        acc[0] = acc[0] * own_part + turned[2].astype(jnp.float32) * other_part
+
     halves = out_ref.shape[1]
     for h in range(heads):
-        lines = slice(h * BLK, (h + 1) * BLK)
-        result = (acc[lines, :] / norm[lines, :]).astype(jnp.bfloat16)
+        part = slice(h * BLK, (h + 1) * BLK)
+        result = jnp.transpose(acc[0, :, part] / norm[0, :, part]).astype(jnp.bfloat16)
         for p in range(BLK // halves):
             out_ref[p, :, h * HEAD_DIM : (h + 1) * HEAD_DIM] = result[p * halves : (p + 1) * halves]
+
+    def finish():
+        for kz in range(layers):
+            for e in range(plane):
+                if e or kz not in (0, layers - 1):
+                    block_copy(kz, e).wait_send()
+
+        @pl.when(paired == 0)
+        def _():
+            block_copy(layers - 1, 0).wait_send()
+
+    return finish
 
 
 def layer_kernel(
@@ -248,10 +361,11 @@
     down_buf,
     held,
     near,
-    heads_first,
+    turned,
     top,
     norm,
     acc,
+    stats,
     att_ref,
     att_buf,
     part,
@@ -282,6 +396,8 @@
     near_recv,
     block_send,
     block_recv,
+    swap_send,
+    swap_recv,
     att_send,
     att_recv,
     rs_pair_send,
@@ -503,7 +619,7 @@
         for j in range(steps - spare):
             down_copy(j).start()
 
-    attention(
+    finish = attention(
         rows,
         cols,
         local_blocks,
@@ -516,15 +632,18 @@
         att_ref,
         held,
         near,
-        heads_first,
+        turned,
         top,
         norm,
         acc,
+        stats,
         near_sem,
         near_send,
         near_recv,
         block_send,
         block_recv,
+        swap_send,
+        swap_recv,
     )
     for q in range(NC):
         for k in range(1, cols):
@@ -570,6 +689,7 @@
     ag_forward(0)
     rs_lines_start(0, 2)
 
+    finish()
     chunks = NC * steps
 
     def stage_when(i, stage):
@@ -762,10 +882,11 @@
             held(STEPS, wide, width),
             held(devices, 2, BLK, HEAD_DIM),
             held(cols, 2, BLK, HEAD_DIM),
-            held(lines, HEAD_DIM),
-            pltpu.VMEM((lines, HEAD_DIM), jnp.float32),
-            pltpu.VMEM((lines, HEAD_DIM), jnp.float32),
-            pltpu.VMEM((lines, HEAD_DIM), jnp.float32),
+            held(3, HEAD_DIM, lines),
+            pltpu.VMEM((2, 1, lines), jnp.float32),
+            pltpu.VMEM((2, 1, lines), jnp.float32),
+            pltpu.VMEM((2, HEAD_DIM, lines), jnp.float32),
+            pltpu.VMEM((2, 2, lines), jnp.float32),
             held(BLK // tokens, tokens, inner),
             held(NC, cols, 2, toks, inner),
             held(NC, row_lines, 2, toks, width),
@@ -791,11 +912,13 @@
             dma((STEPS,)),
             dma((STEPS,)),
             dma((inner // wide,)),
-            dma((3,)),
+            dma((2,)),
             dma((cols - 1,)),
             dma((cols - 1,)),
             dma((devices,)),
             dma((devices,)),
+            dma((3,)),
+            dma((3,)),
             dma((NC, cols - 1)),
             dma((NC, cols - 1)),
             dma((2, NC)),
@@ -814,7 +937,7 @@
             dma((4, SLOTS, col_lines - 1)),
         ],
         compiler_params=pltpu.CompilerParams(
-            collective_id=0, has_side_effects=True, vmem_limit_bytes=66 * 1000 * 1000
+            collective_id=0, has_side_effects=True, vmem_limit_bytes=67 * 1000 * 1000
         ),
     )(
         queries,

time: 203 us -> 198 us (0.975)
  Pallas kernels: 200 us -> 195 us
    pallas_call x1, Pallas kernels: 195 us -> 190 us  [layer_call(): pl.pallas_call(functools.partial(layer_kernel, cols, rows, local_blocks),...]
where the time goes in v4:
time: 198 us
  Pallas kernels  195 us (98%)
  other arithmetic  3.22 us (2%)
    pallas_call x1, Pallas kernels, layer_call(): pl.pallas_call(functools.partial(layer_kernel, cols, rows, local_blocks),...  190 us
    pallas_call x1, Pallas kernels, gather_blocks(): pl.pallas_call(gather_kernel, out_shape=jax.ShapeDtypeStruct((devices, 2,...  4.4 us

profile of v4, /device:TPU:0, one launch (start us, length us, event | category | flops | bytes accessed | tf_op | source)
XLA Modules:
  0.0 197.8 jit_solution(13987296693393026535)
XLA Ops:
  0.0 1.5 fusion.2.rows_ref
  1.5 4.4 %shard_map.118.block_ref = bf16[32,2,128,128]{3,2,1,0:T(8,128)(2,1)} custom-call(s32[4,8]{1,0:T(4,128)} %fusion.2.rows_ref, bf16[8,1024,128]{2,1,0:T(8,128)(2,1)} %keys_ref.1, bf16[8,1024,128]{2,1,0:T(8,128)(2,1)} %values_ref.1), custom_call_target="tpu_custom_call" | custom-call | tf_op jit(solution)/shard_map/pallas_call | solution.py:46
  5.9 190.1 %shard_map.119 = f32[4,16,2048]{2,1,0:T(8,128)} custom-call(bf16[128,1024]{1,0:T(8,128)(2,1)} %query_ref.1, bf16[32,2,128,128]{3,2,1,0:T(8,128)(2,1)} %shard_map.118.block_ref, s32[4,8,16]{2,1,0:T(8,128)} %lists_ref.1, bf16[8,128,128]{2,1,0:T(8,128)(2,1)} %near_key_ref.1, bf16[8,128,128]{2,1,0:T(8,128)(2,1)} %near_value_ref.1, bf16[1024,2048]{1,0:T(8,128)(2,1)} %wo_ref.1, ...), custom_call_target="tpu_custom_call" | custom-call | tf_op jit(solution)/shard_map/pallas_call | solution.py:874
  196.0 1.8 convert_element_type.6

commit v5 on v4

--- a/solution.py
+++ b/solution.py
@@ -375,6 +375,7 @@
     stream,
     square_own,
     square_buf,
+    factors,
     pieces,
     gate_part,
     up_part,
@@ -406,6 +407,8 @@
     rs_line_recv,
     square_send,
     square_recv,
+    factor_send,
+    factor_recv,
     ag_line_send,
     ag_line_recv,
     ag_pair_send,
@@ -535,6 +538,10 @@
         square_own[q] = jnp.broadcast_to(squares, (toks, 128))
         for k in range(1, cols):
             square_copy(q, k).start()
+        pieces[q, depth_me, core] = (value * gain_ref[...].astype(jnp.float32)[None, :]).astype(jnp.bfloat16)
+        for k in range(1, row_lines):
+            ag_line(q, k).start()
+        ag_pair(q, 0).start()
 
     def ag_line(q, k):
         return remote(
@@ -557,18 +564,41 @@
             row_other,
         )
 
-    def norm_step(q):
+    def factor_copy(q, k):
+        return remote(
+            factors.at[q, core],
+            factors.at[q, core],
+            factor_send.at[q, k - 1],
+            factor_recv.at[q, core],
+            "row",
+            flipped(row, k),
+        )
+
+    def factor_step(q):
         squares = square_own[q]
         for k in range(1, cols):
             square_copy(q, k).wait()
             squares = squares + square_buf[q, k - 1]
-        factor = lax.rsqrt(squares / (width * cols) + 1e-05)[:, :1]
-        pieces[q, depth_me, core] = (stream[q] * factor * gain_ref[...].astype(jnp.float32)[None, :]).astype(
-            jnp.bfloat16
-        )
-        for k in range(1, row_lines):
-            ag_line(q, k).start()
-        ag_pair(q, 0).start()
+
+        @pl.when(depth_me == col)
+        def _():
+            factors[q, core] = lax.rsqrt(squares / (width * cols) + 1e-05)
+            for k in range(1, rows):
+                factor_copy(q, k).start()
+
+    def factor_wait(q):
+        for c in range(2):
+
+            @pl.when(row != 2 * col + c)
+            def _():
+                pltpu.make_async_copy(factors.at[q, c], factors.at[q, c], factor_recv.at[q, c]).wait()
+
+    def factor_finish():
+        @pl.when(depth_me == col)
+        def _():
+            for q in range(NC):
+                for k in range(1, rows):
+                    factor_copy(q, k).wait_send()
 
     def ag_forward(q):
         for k in range(1, row_lines):
@@ -677,15 +707,15 @@
     rs_middle(0, 1)
     rs_lines_start(0, 1)
     stream_step(0)
-    norm_step(0)
     stream_step(1)
-    norm_step(1)
+    factor_step(0)
     for q in range(2, NC):
         project(q)
     for j in range(steps - spare, steps):
         down_copy(j).start()
     for q in range(2, NC):
         rs_middle(0, q)
+    factor_step(1)
     ag_forward(0)
     rs_lines_start(0, 2)
 
@@ -749,7 +779,15 @@
             for k in range(1, col_lines):
                 gate = gate + gate_second[slot, k - 1].astype(jnp.float32)
             up = up_mid[hold, pair_me].astype(jnp.float32) + up_second[slot].astype(jnp.float32)
-            hidden = (gate / (1.0 + jnp.exp(-gate)) * up).astype(jnp.bfloat16)
+            q = step // steps
+
+            @pl.when(lax.rem(step, steps) == 0)
+            def _():
+                factor_wait(q)
+
+            factor = factors[q].reshape(share, 128)[:, :1]
+            gate = gate * factor
+            hidden = (gate / (1.0 + jnp.exp(-gate)) * (up * factor)).astype(jnp.bfloat16)
             left[slot, 0, 0] = hidden[:, :half]
             right[slot, 0, 0] = hidden[:, half:]
             for copy in transfers(2, step):
@@ -789,19 +827,19 @@
                     preferred_element_type=jnp.float32,
                 )
 
-        @pl.when((j_now == 1) & (q_now + 2 < NC))
+        @pl.when((j_now == 5) & (q_now + 2 < NC))
         def _():
             stream_step(q_now + 2)
 
-        @pl.when((j_now == 2) & (q_now + 2 < NC))
-        def _():
-            norm_step(q_now + 2)
-
-        @pl.when((j_now == 2) & (q_now + 3 < NC))
+        @pl.when((j_now == 6) & (q_now + 2 < NC))
+        def _():
+            factor_step(q_now + 2)
+
+        @pl.when((j_now == 5) & (q_now + 3 < NC))
         def _():
             rs_lines_start(0, q_now + 3)
 
-        @pl.when((j_now == 4) & (q_now + 1 < NC))
+        @pl.when((j_now == 5) & (q_now + 1 < NC))
         def _():
             ag_forward(q_now + 1)
 
@@ -832,6 +870,7 @@
         return carry
 
     lax.fori_loop(0, chunks + LAGS[4], iteration, 0)
+    factor_finish()
     rs_middle(1, NC - 1)
     rs_lines_start(1, NC - 1)
     out_ref[NC - 1] = stream[NC - 1] + rs_finish(1, NC - 1)
@@ -896,6 +935,7 @@
             pltpu.VMEM((NC, toks, width), jnp.float32),
             pltpu.VMEM((NC, toks, 128), jnp.float32),
             pltpu.VMEM((NC, cols - 1, toks, 128), jnp.float32),
+            pltpu.VMEM((NC, 2, toks, 128), jnp.float32),
             held(NC, row_lines, 2, toks, depth),
             held(HOLD, 2, col_lines, share, wide),
             held(HOLD, col_lines, 2, share, wide),
@@ -927,6 +967,8 @@
             dma((2, NC, row_lines - 1)),
             dma((NC, cols - 1)),
             dma((NC, cols - 1)),
+            dma((NC, rows - 1)),
+            dma((NC, 2)),
             dma((NC, row_lines - 1)),
             dma((NC, row_lines - 1)),
             dma((NC, row_lines)),

time: 198 us -> 191 us (0.965)
  Pallas kernels: 195 us -> 188 us
    pallas_call x1, Pallas kernels: 190 us -> 183 us  [layer_call(): pl.pallas_call(functools.partial(layer_kernel, cols, rows, local_blocks),...]
where the time goes in v5:
time: 191 us
  Pallas kernels  188 us (98%)
  other arithmetic  3.22 us (2%)
    pallas_call x1, Pallas kernels, layer_call(): pl.pallas_call(functools.partial(layer_kernel, cols, rows, local_blocks),...  183 us
    pallas_call x1, Pallas kernels, gather_blocks(): pl.pallas_call(gather_kernel, out_shape=jax.ShapeDtypeStruct((devices, 2,...  4.4 us

profile of v5, /device:TPU:0, one launch (start us, length us, event | category | flops | bytes accessed | tf_op | source)
XLA Modules:
  0.0 190.9 jit_solution(16961512331580795233)
XLA Ops:
  0.0 1.5 fusion.2.rows_ref
  1.5 4.4 %shard_map.118.block_ref = bf16[32,2,128,128]{3,2,1,0:T(8,128)(2,1)} custom-call(s32[4,8]{1,0:T(4,128)} %fusion.2.rows_ref, bf16[8,1024,128]{2,1,0:T(8,128)(2,1)} %keys_ref.1, bf16[8,1024,128]{2,1,0:T(8,128)(2,1)} %values_ref.1), custom_call_target="tpu_custom_call" | custom-call | tf_op jit(solution)/shard_map/pallas_call | solution.py:46
  5.9 183.3 %shard_map.119 = f32[4,16,2048]{2,1,0:T(8,128)} custom-call(bf16[128,1024]{1,0:T(8,128)(2,1)} %query_ref.1, bf16[32,2,128,128]{3,2,1,0:T(8,128)(2,1)} %shard_map.118.block_ref, s32[4,8,16]{2,1,0:T(8,128)} %lists_ref.1, bf16[8,128,128]{2,1,0:T(8,128)(2,1)} %near_key_ref.1, bf16[8,128,128]{2,1,0:T(8,128)(2,1)} %near_value_ref.1, bf16[1024,2048]{1,0:T(8,128)(2,1)} %wo_ref.1, ...), custom_call_target="tpu_custom_call" | custom-call | tf_op jit(solution)/shard_map/pallas_call | solution.py:913
  189.2 1.8 convert_element_type.6

commit v6 on v5

--- a/solution.py
+++ b/solution.py
@@ -715,9 +715,9 @@
         down_copy(j).start()
     for q in range(2, NC):
         rs_middle(0, q)
+    rs_lines_start(0, 2)
     factor_step(1)
     ag_forward(0)
-    rs_lines_start(0, 2)
 
     finish()
     chunks = NC * steps
@@ -1018,8 +1018,9 @@
     device_count = row_count * col_count
     my_index = row_index * col_count + col_index
     local_blocks = cache_keys.shape[1] // BLK
-    matched = block_lists // local_blocks == my_index
-    block_rows = jnp.sum(jnp.where(matched, block_lists % local_blocks, 0), axis=2)
+    within = block_lists - my_index * local_blocks
+    matched = (within >= 0) & (within < local_blocks)
+    block_rows = jnp.sum(jnp.where(matched, within, 0), axis=2)
     blocks = gather_blocks(block_rows, cache_keys, cache_values, device_count)
     return layer_call(
         queries,

time: 191 us -> 191 us (level)
  no operation moved by 1% of the time
where the time goes in v6:
time: 191 us
  Pallas kernels  188 us (98%)
  other arithmetic  3.22 us (2%)
    pallas_call x1, Pallas kernels, layer_call(): pl.pallas_call(functools.partial(layer_kernel, cols, rows, local_blocks),...  183 us
    pallas_call x1, Pallas kernels, gather_blocks(): pl.pallas_call(gather_kernel, out_shape=jax.ShapeDtypeStruct((devices, 2,...  4.4 us

profile of v6, /device:TPU:0, one launch (start us, length us, event | category | flops | bytes accessed | tf_op | source)
XLA Modules:
  0.0 190.9 jit_solution(2022658217841212848)
XLA Ops:
  0.0 1.4 select_reduce_fusion.rows_ref
  1.4 4.4 %shard_map.118.block_ref = bf16[32,2,128,128]{3,2,1,0:T(8,128)(2,1)} custom-call(s32[4,8]{1,0:T(4,128)} %select_reduce_fusion.rows_ref, bf16[8,1024,128]{2,1,0:T(8,128)(2,1)} %keys_ref.1, bf16[8,1024,128]{2,1,0:T(8,128)(2,1)} %values_ref.1), custom_call_target="tpu_custom_call" | custom-call | tf_op jit(solution)/shard_map/pallas_call | solution.py:46
  5.9 183.2 %shard_map.119 = f32[4,16,2048]{2,1,0:T(8,128)} custom-call(bf16[128,1024]{1,0:T(8,128)(2,1)} %query_ref.1, bf16[32,2,128,128]{3,2,1,0:T(8,128)(2,1)} %shard_map.118.block_ref, s32[4,8,16]{2,1,0:T(8,128)} %lists_ref.1, bf16[8,128,128]{2,1,0:T(8,128)(2,1)} %near_key_ref.1, bf16[8,128,128]{2,1,0:T(8,128)(2,1)} %near_value_ref.1, bf16[1024,2048]{1,0:T(8,128)(2,1)} %wo_ref.1, ...), custom_call_target="tpu_custom_call" | custom-call | tf_op jit(solution)/shard_map/pallas_call | solution.py:913
  189.1 1.8 convert_element_type.6
